TPU v7x, 512 devices: a whole 4x4x16 slice. The times are simulated.
512 devices in a mesh: chan: 16 (over y, x_lo, core), slab: 32 (over z, x_hi).
Axes of the slice: x: 4 (x_hi: 2, x_lo: 2; x = x_hi * 2 + x_lo), y: 4, z: 16, core: 2. Of those that a mesh axis runs over, the one named last changes fastest.
Arguments:
- capture: bfloat16 [2, 2, 32, 3072, 2048], P(None, None, 'slab', 'chan'), may hold values from -6 to 6
- chirp_rates: float32 [2048], P('chan'), may hold values from 64 to 480
- phase_bin: int32 [98304], P('slab'), may hold values from 0 to 1023, as said below
- sub_id: int32 [98304], P('slab'), may hold values from 0 to 1, as said below
Outputs:
- folded: float32 [2048, 2, 1024], P(('chan', 'slab'))
Inputs may be any that keep to these rules, and one draw needn't show every extreme that they name: phase_bin[t] = floor(1024 * frac((64 t + q) / m)) for an odd whole number m from 16384 to 65536 and a whole number q, both drawn with the window. `sub_id`: nondecreasing in time; it changes only between sample 98304 // 4 and sample 3 * 24576.
All inputs are finite; a program needn't handle non-finite values.
Results may differ from a plain program's by a relative error of at most 0.015.
Values may be sent and summed in bfloat16 or wider, within the bound.
No kernel may reach another device: no remote copies, remote signals or barrier semaphores. Data moves between devices by JAX's collectives and lax.ppermute only.
A program may use at most 64 MiB of HBM per device.

v0:
```python
import math

import jax
import jax.numpy as jnp
from jax import lax
from jax.sharding import PartitionSpec as P

RADIX = 64
BINS = 1024
NSUB = 2
NFFT = 4096
NTAP = 1024


def passed_along(shard, axis, by):
    length = lax.axis_size(axis)
    pairs = [(i, i + by) for i in range(length) if 0 <= i + by < length]
    return lax.ppermute(shard, axis, pairs)


def transform_tables():
    indices = jnp.arange(RADIX, dtype=jnp.int32)
    small = indices[:, None] * indices[None, :] % RADIX
    angles = 2.0 * math.pi / RADIX * small.astype(jnp.float32)
    cosine = jnp.cos(angles)
    sine = jnp.sin(angles)
    forward = jnp.stack(
        [jnp.stack([cosine, -sine], axis=1), jnp.stack([sine, cosine], axis=1)], axis=0
    ).astype(jnp.bfloat16)
    inverse = jnp.stack(
        [jnp.stack([cosine, sine], axis=1), jnp.stack([-sine, cosine], axis=1)], axis=0
    ).astype(jnp.bfloat16)
    large = indices[:, None] * indices[None, :] % NFFT
    twist = 2.0 * math.pi / NFFT * large.astype(jnp.float32)
    return (forward, inverse, jnp.cos(twist)[:, :, None], jnp.sin(twist)[:, :, None])


def chirp_table(rates_here):
    indices = jnp.arange(RADIX, dtype=jnp.int32)
    spectral = indices[:, None] + RADIX * indices[None, :]
    offset = ((spectral + NFFT // 2) % NFFT).astype(jnp.float32) / NFFT
    turns = rates_here[None, None, :] * (offset * offset)[:, :, None]
    phase = 2.0 * math.pi * (turns - jnp.floor(turns))
    return (jnp.cos(phase), jnp.sin(phase))


def detect_block(turned, tables):
    forward, inverse, twid_cos, twid_sin, chirp_cos, chirp_sin = tables
    pols = turned.shape[0]
    span = turned.shape[3]
    width = turned.shape[4]
    tail_rows = turned[:, :, :, span - NTAP :, :]
    previous = passed_along(tail_rows, "slab", 1)
    block_data = jnp.concatenate([previous, turned], axis=3).reshape(pols, 2, RADIX, RADIX, width)
    section_one = jnp.einsum(
        "rask,prabc->pskbc", forward, block_data, preferred_element_type=jnp.float32
    )
    real_part, imag_part = (section_one[:, 0], section_one[:, 1])
    middle = jnp.stack(
        [real_part * twid_cos + imag_part * twid_sin, imag_part * twid_cos - real_part * twid_sin],
        axis=1,
    ).astype(jnp.bfloat16)
    spectrum = jnp.einsum("rbsw,prkbc->pskwc", forward, middle, preferred_element_type=jnp.float32)
    real_part, imag_part = (spectrum[:, 0], spectrum[:, 1])
    filtered = jnp.stack(
        [
            real_part * chirp_cos + imag_part * chirp_sin,
            imag_part * chirp_cos - real_part * chirp_sin,
        ],
        axis=1,
    ).astype(jnp.bfloat16)
    section_three = jnp.einsum(
        "rwsa,prkwc->pskac", inverse, filtered, preferred_element_type=jnp.float32
    )
    real_part, imag_part = (section_three[:, 0], section_three[:, 1])
    back = jnp.stack(
        [real_part * twid_cos - imag_part * twid_sin, imag_part * twid_cos + real_part * twid_sin],
        axis=1,
    ).astype(jnp.bfloat16)
    section_four = jnp.einsum(
        "rksb,prkac->psbac", inverse, back, preferred_element_type=jnp.float32
    )
    kept = section_four[:, :, NTAP // RADIX :] * (1.0 / NFFT)
    voltage = kept.reshape(pols, 2, span, width)
    return jnp.sum(voltage * voltage, axis=1)


def shards(capture, chirp_rates, phase_bin, sub_id):
    forward, inverse, twid_cos, twid_sin = transform_tables()
    chirp_cos, chirp_sin = chirp_table(chirp_rates)
    tables = (forward, inverse, twid_cos, twid_sin, chirp_cos, chirp_sin)
    turned = lax.all_to_all(capture, "chan", split_axis=4, concat_axis=3, tiled=True)
    detected = detect_block(turned, tables)
    power = jnp.sum(detected, axis=0).astype(jnp.bfloat16)
    span = power.shape[0]
    onehot = (phase_bin[:, None] == jnp.arange(BINS, dtype=jnp.int32)[None, :]).astype(jnp.bfloat16)
    sub_masks = (sub_id[None, :] == jnp.arange(NSUB, dtype=jnp.int32)[:, None]).astype(jnp.bfloat16)
    weighted = sub_masks[:, :, None] * power[None, :, :]
    slab_count = lax.axis_size("slab")
    summed = lax.psum_scatter(
        jnp.einsum("stc,tb->csb", weighted, onehot, preferred_element_type=jnp.float32).astype(
            jnp.bfloat16
        ),
        "slab",
        scatter_dimension=0,
        tiled=True,
    ).astype(jnp.float32)
    scale = NSUB * BINS / (4.0 * span * slab_count)
    return summed * scale


def solution(mesh):
    placed = (P(None, None, "slab", "chan", None), P("chan"), P("slab"), P("slab"))
    return jax.shard_map(
        shards,
        mesh=mesh,
        in_specs=placed,
        out_specs=P(("chan", "slab"), None, None),
        check_vma=False,
    )
```

profile of v0, /device:TPU:16, one launch (start us, length us, event | category | flops | bytes accessed | tf_op | source)
XLA Modules:
  0.0 459.4 jit_solution(16345917757796049255)
XLA Ops:
  6.5 11.0 %copy.52 = bf16[2,2,1,192,2048]{3,1,2,0,4:T(2,128)(2,1)} copy(bf16[2,2,1,192,2048]{4,3,2,1,0:T(8,128)(2,1)} %param.4) | data formatting | bytes 6291456 | tf_op args[0]
  17.5 10.0 %all-to-all-start = ((bf16[2,2,1,192,2048]{3,1,2,0,4:T(2,128)(2,1)}), bf16[2,2,1,192,2048]{3,1,2,0,4:T(2,128)(2,1)}, u32[]{:S(2)}, u32[]{:S(2)}) async-start(bf16[2,2,1,192,2048]{3,1,2,0,4:T(2,128)(2,1)} %copy.52), calls=%async_computation | async-start | bytes 8388608 | tf_op jit(solution)/shard_map/all_to_all | solution.py:92
  27.6 0.0 all-reduce.3.cloned.1.call-start
  27.6 0.1 fusion.71
  27.8 0.2 negate_convert_fusion
  27.9 0.1 fusion.61
  28.0 47.3 %all-to-all-done = bf16[2,2,1,192,2048]{3,1,2,0,4:T(2,128)(2,1)} async-done(((bf16[2,2,1,192,2048]{3,1,2,0,4:T(2,128)(2,1)}), bf16[2,2,1,192,2048]{3,1,2,0,4:T(2,128)(2,1)}, u32[]{:S(2)}, u32[]{:S(2)}) %all-to-all-start) | async-done | bytes 3145760 | tf_op jit(solution)/shard_map/all_to_all | solution.py:92
  75.4 9.4 %copy.76 = bf16[2,2,1,192,16,128]{5,3,4,1,0,2:T(8,128)(2,1)S(1)} copy(bf16[2,2,1,192,16,128]{3,1,0,5,4,2:T(2,128)(2,1)} %bitcast.1) | data formatting | bytes 6291456 | tf_op jit(solution)/shard_map/all_to_all | solution.py:92
  84.8 1.0 slice.32
  85.9 2.3 collective-permute-start
  88.2 0.1 fusion.68
  88.3 0.1 copy.58
  88.4 7.5 %fusion.34 = (f32[64,64,128]{2,1,0:T(8,128)S(1)}, f32[64,64,128]{2,1,0:T(8,128)S(1)}) fusion(f32[64,64]{1,0:T(8,128)S(1)} %copy.58, f32[128]{0:T(128)S(1)} %copy-done.1), kind=kLoop, calls=%fused_computation.37 | loop fusion | flops 2097152 | bytes 4211200 | tf_op jit(solution)/shard_map/cos | solution.py:44
  96.0 14.1 %collective-permute-done = bf16[2,2,1,1024,128]{4,3,1,0,2:T(8,128)(2,1)} collective-permute-done((bf16[2,2,1,1024,128]{4,3,1,0,2:T(8,128)(2,1)}, bf16[2,2,1,1024,128]{4,3,1,0,2:T(8,128)(2,1)}, u32[]{:S(2)}, u32[]{:S(2)}) %collective-permute-start) | collective-permute-done | bytes 1048608 | tf_op jit(solution)/shard_map/ppermute | solution.py:18
  110.1 1.5 pad_maximum_fusion
  111.6 3.2 fusion.20
  114.8 1.8 add_convert_fusion.2
  116.5 0.4 maximum_bitcast_fusion
  117.0 3.2 fusion.23
  120.2 1.6 add_convert_fusion.1
  121.8 1.3 fusion.26
  123.1 4.9 %copy.94 = f32[2,64,128,2,64]{2,1,3,4,0:T(8,128)S(1)} copy(f32[2,64,128,2,64]{2,4,3,1,0:T(8,128)S(1)} %fusion.26) | data formatting | bytes 16777216 | tf_op jit(solution)/shard_map/rwsa,prkwc->pskac/dot_general | solution.py:72
  127.9 2.0 subtract_convert_fusion
  129.9 1.3 fusion.29
  131.2 0.8 fusion.4
  132.0 0.2 copy.62
  132.2 2.4 fusion.41
  134.6 1.1 copy.63
  135.8 0.0 all-reduce.3.cloned.1.call-update
  135.8 1.3 dynamic-slice
  137.7 313.4 %all-reduce.3.cloned.1.call-done = bf16[128,2,1024]{2,1,0:T(2,128)(2,1)} async-done(((bf16[128,2,1024]{2,1,0:T(2,128)(2,1)}), bf16[128,2,1024]{2,1,0:T(2,128)(2,1)}) %all-reduce.3.cloned.1.call-update) | async-done | bytes 524304
  451.2 1.3 convert_multiply_fusion
  (9 shorter events, 0.1 us)
Async XLA Ops:
  17.5 57.8 %all-to-all-start = ((bf16[2,2,1,192,2048]{3,1,2,0,4:T(2,128)(2,1)}), bf16[2,2,1,192,2048]{3,1,2,0,4:T(2,128)(2,1)}, u32[]{:S(2)}, u32[]{:S(2)}) async-start(bf16[2,2,1,192,2048]{3,1,2,0,4:T(2,128)(2,1)} %copy.52), calls=%async_computation | async-start | bytes 8388608 | tf_op jit(solution)/shard_map/all_to_all | solution.py:92
  27.6 423.6 %all-reduce.3.cloned.1.call-start = ((), (), s32[]{:S(2)}) async-start(), calls=%async_computation.1 | async-start | bytes 1048576
  75.4 13.0 %copy-start.1 = (f32[128]{0:T(128)S(1)}, f32[128]{0:T(128)}, u32[]{:S(2)}) copy-start(f32[128]{0:T(128)} %param.5) | copy-start | bytes 1540
  84.8 11.1 %copy-start = (s32[3072]{0:T(1024)S(1)}, s32[3072]{0:T(1024)}, u32[]{:S(2)}) copy-start(s32[3072]{0:T(1024)} %param.7) | copy-start | bytes 36868
  85.9 24.2 %collective-permute-start = (bf16[2,2,1,1024,128]{4,3,1,0,2:T(8,128)(2,1)}, bf16[2,2,1,1024,128]{4,3,1,0,2:T(8,128)(2,1)}, u32[]{:S(2)}, u32[]{:S(2)}) collective-permute-start(bf16[2,2,1,1024,128]{4,3,1,0,2:T(8,128)(2,1)} %slice.32), channel_id=1, source_target_pairs={{0,1},{1,2},{2,3},{3,4},{4,5},{5,6},{6,7},{7,8},{8,9},{9,10},{10,1... | collective-permute-start | bytes 3145736 | tf_op jit(solution)/shard_map/ppermute | solution.py:18
  131.2 1.0 copy-start.2
Sparse Core Ops, SparseCore 0:
  135.9 315.2 all-reduce.2
where the time goes:
time: 460 us; the launch traced here: 459 us
  waiting for transfers between devices  375 us (82%)
  local copies, waits for them, and re-layouts  29 us (6%)
  other arithmetic  17.4 us (4%)
  between operations  14.2 us (3%)
  starting transfers between devices  12.4 us (3%)
  matrix products  11.4 us (2%)
    unnamed x2, waiting for transfers between devices  313 us
    all_to_all x1, waiting for transfers between devices, shards(): lax.all_to_all(capture, 'chan', split_axis=4, concat_axis=3, tiled=True)  47.3 us
    ppermute x1, waiting for transfers between devices, passed_along(): return lax.ppermute(shard, axis, pairs)  14.1 us
    unnamed x8, local copies, waits for them, and re-layouts  12.3 us
    all_to_all x1, starting transfers between devices, shards(): lax.all_to_all(capture, 'chan', split_axis=4, concat_axis=3, tiled=True)  10 us
    all_to_all x1, local copies, waits for them, and re-layouts, shards(): lax.all_to_all(capture, 'chan', split_axis=4, concat_axis=3, tiled=True)  9.43 us
  transfers between devices with their start and end apart: 3, of which 3 were waited for; matrix products, arithmetic and copies ran while one was open for 2% of the time, Pallas kernels for 0%

commit v1 on v0

--- a/solution.py
+++ b/solution.py
@@ -97,14 +97,13 @@
     sub_masks = (sub_id[None, :] == jnp.arange(NSUB, dtype=jnp.int32)[:, None]).astype(jnp.bfloat16)
     weighted = sub_masks[:, :, None] * power[None, :, :]
     slab_count = lax.axis_size("slab")
-    summed = lax.psum_scatter(
-        jnp.einsum("stc,tb->csb", weighted, onehot, preferred_element_type=jnp.float32).astype(
-            jnp.bfloat16
-        ),
-        "slab",
-        scatter_dimension=0,
-        tiled=True,
-    ).astype(jnp.float32)
+    partial = jnp.einsum(
+        "stc,tb->csb", weighted, onehot, preferred_element_type=jnp.float32
+    ).astype(jnp.bfloat16)
+    channels = partial.shape[0] // slab_count
+    pieces = partial.reshape(slab_count, channels, NSUB, BINS)
+    pieces = lax.all_to_all(pieces, "slab", split_axis=0, concat_axis=0, tiled=True)
+    summed = jnp.sum(pieces.astype(jnp.float32), axis=0)
     scale = NSUB * BINS / (4.0 * span * slab_count)
     return summed * scale
 

time: 460 us -> 184 us (0.40)
  the two profiles are of different devices: /device:TPU:16 before, /device:TPU:6 now
where the time goes in v1:
time: 184 us; the launch traced here: 183 us
  waiting for transfers between devices  67 us (36%)
  blocking collectives  48.9 us (27%)
  local copies, waits for them, and re-layouts  28.1 us (15%)
  other arithmetic  16.9 us (9%)
  matrix products  11.5 us (6%)
  starting transfers between devices  10.6 us (6%)
    all_to_all x1, blocking collectives, shards(): lax.all_to_all(pieces, 'slab', split_axis=0, concat_axis=0, tiled=True)  48.9 us
    all_to_all x1, waiting for transfers between devices, shards(): lax.all_to_all(capture, 'chan', split_axis=4, concat_axis=3, tiled=True)  48.7 us
    ppermute x1, waiting for transfers between devices, passed_along(): return lax.ppermute(shard, axis, pairs)  18.2 us
    unnamed x7, local copies, waits for them, and re-layouts  11.1 us
    all_to_all x1, local copies, waits for them, and re-layouts, shards(): lax.all_to_all(capture, 'chan', split_axis=4, concat_axis=3, tiled=True)  9.43 us
    cos x1, other arithmetic, chirp_table(): return (jnp.cos(phase), jnp.sin(phase))  7.5 us
    all_to_all x1, starting transfers between devices, shards(): lax.all_to_all(capture, 'chan', split_axis=4, concat_axis=3, tiled=True)  5.94 us
    another operation x5, other arithmetic  5.92 us
  transfers between devices with their start and end apart: 2, of which 2 were waited for; matrix products, arithmetic and copies ran while one was open for 4% of the time, Pallas kernels for 0%

profile of v1, /device:TPU:6, one launch (start us, length us, event | category | flops | bytes accessed | tf_op | source)
XLA Modules:
  0.0 183.3 jit_solution(4213566814470422966)
XLA Ops:
  0.0 11.0 %copy.58 = bf16[2,2,1,192,2048]{3,1,2,0,4:T(2,128)(2,1)} copy(bf16[2,2,1,192,2048]{4,3,2,1,0:T(8,128)(2,1)} %param.4) | data formatting | bytes 6291456 | tf_op args[0]
  11.0 5.9 %all-to-all-start = ((bf16[2,2,1,192,2048]{3,1,2,0,4:T(2,128)(2,1)}), bf16[2,2,1,192,2048]{3,1,2,0,4:T(2,128)(2,1)}, u32[]{:S(2)}, u32[]{:S(2)}) async-start(bf16[2,2,1,192,2048]{3,1,2,0,4:T(2,128)(2,1)} %copy.58), calls=%async_computation | async-start | bytes 8388608 | tf_op jit(solution)/shard_map/all_to_all | solution.py:92
  17.0 0.1 fusion.56
  17.1 0.2 negate_convert_fusion
  17.3 0.1 fusion.46
  17.4 48.7 %all-to-all-done = bf16[2,2,1,192,2048]{3,1,2,0,4:T(2,128)(2,1)} async-done(((bf16[2,2,1,192,2048]{3,1,2,0,4:T(2,128)(2,1)}), bf16[2,2,1,192,2048]{3,1,2,0,4:T(2,128)(2,1)}, u32[]{:S(2)}, u32[]{:S(2)}) %all-to-all-start) | async-done | bytes 3145760 | tf_op jit(solution)/shard_map/all_to_all | solution.py:92
  66.2 9.4 %copy.86 = bf16[2,2,1,192,16,128]{5,3,4,1,0,2:T(8,128)(2,1)S(1)} copy(bf16[2,2,1,192,16,128]{3,1,0,5,4,2:T(2,128)(2,1)} %bitcast) | data formatting | bytes 6291456 | tf_op jit(solution)/shard_map/all_to_all | solution.py:92
  75.6 1.0 slice.32
  76.6 4.7 %collective-permute-start = (bf16[2,2,1,1024,128]{4,3,1,0,2:T(8,128)(2,1)}, bf16[2,2,1,1024,128]{4,3,1,0,2:T(8,128)(2,1)}, u32[]{:S(2)}, u32[]{:S(2)}) collective-permute-start(bf16[2,2,1,1024,128]{4,3,1,0,2:T(8,128)(2,1)} %slice.32), channel_id=1, source_target_pairs={{0,1},{1,2},{2,3},{3,4},{4,5},{5,6},{6,7},{7,8},{8,9},{9,10},{10,1... | collective-permute-start | bytes 3145736 | tf_op jit(solution)/shard_map/ppermute | solution.py:18
  81.3 0.1 fusion.53
  81.5 7.5 %fusion.32 = (f32[64,64,128]{2,1,0:T(8,128)S(1)}, f32[64,64,128]{2,1,0:T(8,128)S(1)}) fusion(f32[64,64]{1,0:T(8,128)S(1)} %copy.64, f32[128]{0:T(128)S(1)} %copy-done.1), kind=kLoop, calls=%fused_computation.36 | loop fusion | flops 2097152 | bytes 4211200 | tf_op jit(solution)/shard_map/cos | solution.py:44
  89.1 18.2 %collective-permute-done = bf16[2,2,1,1024,128]{4,3,1,0,2:T(8,128)(2,1)} collective-permute-done((bf16[2,2,1,1024,128]{4,3,1,0,2:T(8,128)(2,1)}, bf16[2,2,1,1024,128]{4,3,1,0,2:T(8,128)(2,1)}, u32[]{:S(2)}, u32[]{:S(2)}) %collective-permute-start) | collective-permute-done | bytes 1048608 | tf_op jit(solution)/shard_map/ppermute | solution.py:18
  107.3 1.5 pad_maximum_fusion
  108.8 3.2 %fusion.18 = f32[2,2,64,64,128]{4,2,1,3,0:T(8,128)S(1)} fusion(bf16[2,2,64,64,128,1]{4,3,2,1,0,5:T(8,128)(2,1)S(1)} %bitcast.87, bf16[1,64,2,64]{1,3,0,2:T(8,128)(2,1)S(1)} %get-tuple-element.14, bf16[1,64,2,64]{1,3,0,2:T(8,128)(2,1)S(1)} %get-tuple-element.17), kind=kOutput, calls=%fused_computation.29 | convolution fusion | flops 536936448 | bytes 12615680 | tf_op jit(solution)/shard_map/rask,prabc->pskbc/dot_general | solution.py:55
  112.0 1.9 %add_convert_fusion.2 = (bf16[2,1,64,64,128]{4,2,1,3,0:T(8,128)(2,1)S(1)}, bf16[2,1,64,64,128]{4,2,1,3,0:T(8,128)(2,1)S(1)}) fusion(f32[2,2,64,64,128]{4,2,1,3,0:T(8,128)S(1)} %fusion.18, f32[64,64]{0,1:T(8,128)S(1)} %get-tuple-element.21, f32[64,64]{0,1:T(8,128)S(1)} %get-tuple-element.22), kind=kLoop, calls=%fused_computation.28 | loop fusion | flops 8388608 | bytes 12615680 | tf_op jit(solution)/shard_map/convert.12
  114.0 0.4 maximum_bitcast_fusion
  114.4 3.2 %fusion.21 = f32[2,2,64,64,128]{4,3,1,2,0:T(8,128)S(1)} fusion(bf16[2,2,64,64,128,1]{4,2,1,3,0,5:T(8,128)(2,1)S(1)} %maximum_bitcast_fusion, bf16[1,64,2,64]{1,3,0,2:T(8,128)(2,1)S(1)} %get-tuple-element.14, bf16[1,64,2,64]{1,3,0,2:T(8,128)(2,1)S(1)} %get-tuple-element.17), kind=kOutput, calls=%fused_computation.30 | convolution fusion | flops 536936448 | bytes 12615680 | tf_op jit(solution)/shard_map/rbsw,prkbc->pskwc/dot_general | solution.py:63
  117.5 1.7 add_convert_fusion.1
  119.2 1.3 fusion.24
  120.5 4.9 %copy.107 = f32[2,64,128,2,64]{2,1,3,4,0:T(8,128)S(1)} copy(f32[2,64,128,2,64]{2,4,3,1,0:T(8,128)S(1)} %fusion.24) | data formatting | bytes 16777216 | tf_op jit(solution)/shard_map/rwsa,prkwc->pskac/dot_general | solution.py:72
  125.4 2.0 %subtract_convert_fusion = (bf16[2,1,64,64,128]{4,2,1,3,0:T(8,128)(2,1)S(1)}, bf16[2,1,64,64,128]{4,2,1,3,0:T(8,128)(2,1)S(1)}) fusion(f32[2,2,64,64,128]{4,2,1,3,0:T(8,128)S(1)} %bitcast.84, f32[64,64]{0,1:T(8,128)S(1)} %get-tuple-element.21, f32[64,64]{0,1:T(8,128)S(1)} %get-tuple-element.22), kind=kLoop, calls=%fused_computation.24 | loop fusion | flops 8388608 | bytes 12615680 | tf_op jit(solution)/shard_map/convert
  127.4 1.3 fusion.27
  128.7 0.8 fusion.2
  129.5 0.2 copy.68
  129.7 0.3 copy.69
  130.0 0.1 broadcast_multiply_fusion
  130.2 2.6 %fusion = f32[1024,256]{0,1:S(1)} fusion(bf16[3072,256]{0,1:T(8,128)(2,1)S(1)} %bitcast.89, s32[3072]{0:T(1024)S(1)} %copy-done.2), kind=kOutput, calls=%fused_computation.1 | convolution fusion | flops 1613758464 | bytes 2633728
  132.9 0.2 reshape.195
  133.1 0.3 copy.70
  133.3 48.9 %all_to_all.23 = bf16[32,4,2,1024]{3,1,2,0:T(4,128)(2,1)S(1)} all-to-all(bf16[32,4,2,1024]{3,1,2,0:T(4,128)(2,1)S(1)} %copy.70), channel_id=1, replica_groups=mesh['chan'=16,'slab'=32] {'slab'}, dimensions={0} | all-to-all | bytes 1048576 | tf_op jit(solution)/shard_map/all_to_all | solution.py:105
  182.2 0.4 convert_reduce_fusion
  182.6 0.6 copy.73
  (12 shorter events, 0.3 us)
Async XLA Ops:
  11.0 55.1 %all-to-all-start = ((bf16[2,2,1,192,2048]{3,1,2,0,4:T(2,128)(2,1)}), bf16[2,2,1,192,2048]{3,1,2,0,4:T(2,128)(2,1)}, u32[]{:S(2)}, u32[]{:S(2)}) async-start(bf16[2,2,1,192,2048]{3,1,2,0,4:T(2,128)(2,1)} %copy.58), calls=%async_computation | async-start | bytes 8388608 | tf_op jit(solution)/shard_map/all_to_all | solution.py:92
  66.1 15.4 %copy-start.1 = (f32[128]{0:T(128)S(1)}, f32[128]{0:T(128)}, u32[]{:S(2)}) copy-start(f32[128]{0:T(128)} %param.5) | copy-start | bytes 1540
  75.6 13.5 %copy-start = (s32[3072]{0:T(1024)S(1)}, s32[3072]{0:T(1024)}, u32[]{:S(2)}) copy-start(s32[3072]{0:T(1024)} %param.7) | copy-start | bytes 36868
  76.6 30.7 %collective-permute-start = (bf16[2,2,1,1024,128]{4,3,1,0,2:T(8,128)(2,1)}, bf16[2,2,1,1024,128]{4,3,1,0,2:T(8,128)(2,1)}, u32[]{:S(2)}, u32[]{:S(2)}) collective-permute-start(bf16[2,2,1,1024,128]{4,3,1,0,2:T(8,128)(2,1)} %slice.32), channel_id=1, source_target_pairs={{0,1},{1,2},{2,3},{3,4},{4,5},{5,6},{6,7},{7,8},{8,9},{9,10},{10,1... | collective-permute-start | bytes 3145736 | tf_op jit(solution)/shard_map/ppermute | solution.py:18
  129.5 0.7 copy-start.2

commit v2 on v1

v2 whole, which is shorter than its diff:
```python
import functools
import math

import jax
import jax.numpy as jnp
from jax import lax
from jax.experimental import pallas as pl
from jax.experimental.pallas import tpu as pltpu
from jax.sharding import Mesh
from jax.sharding import PartitionSpec as P

RADIX = 64
BINS = 1024
NSUB = 2
NFFT = 4096
NTAP = 1024
LANES = 128
GROUP = 32
QUADS = 4
PAGE = 256
KEYS = NSUB * BINS // PAGE
VMEM = pltpu.VMEM


def real_form(cosine, sine):
    top = jnp.concatenate([cosine, sine], axis=1)
    bottom = jnp.concatenate([-sine, cosine], axis=1)
    return jnp.concatenate([top, bottom], axis=0)


def transform_tables():
    indices = jnp.arange(RADIX, dtype=jnp.int32)
    small = indices[:, None] * indices[None, :] % RADIX
    angles = 2.0 * math.pi / RADIX * small.astype(jnp.float32)
    cosine = jnp.cos(angles).astype(jnp.bfloat16)
    sine = jnp.sin(angles).astype(jnp.bfloat16)
    forward = real_form(cosine, sine)
    inverse = real_form(cosine, -sine)
    first = NTAP // RADIX
    last = jnp.concatenate([inverse[first:RADIX], inverse[RADIX + first :]], axis=0)
    large = indices[:, None] * indices[None, :] % NFFT
    twist = 2.0 * math.pi / NFFT * large.astype(jnp.float32)
    shape = (RADIX, RADIX, LANES)
    twid_cos = jnp.broadcast_to(jnp.cos(twist)[:, :, None], shape).reshape(-1, LANES)
    twid_sin = jnp.broadcast_to(jnp.sin(twist)[:, :, None], shape).reshape(-1, LANES)
    return forward, inverse, last, twid_cos, twid_sin


def chirp_table(rates_here):
    indices = jnp.arange(RADIX, dtype=jnp.int32)
    spectral = indices[:, None] + RADIX * indices[None, :]
    offset = ((spectral + NFFT // 2) % NFFT).astype(jnp.float32) / NFFT
    turns = rates_here[None, None, :] * (offset * offset)[:, :, None]
    phase = 2.0 * math.pi * (turns - jnp.floor(turns))
    return jnp.cos(phase).reshape(-1, LANES), jnp.sin(phase).reshape(-1, LANES)


def iota(shape, axis):
    return lax.broadcasted_iota(jnp.int32, shape, axis)


def dot(a, b):
    return jnp.dot(a, b, preferred_element_type=jnp.float32)


def pack_kernel(groups, x_ref, o_ref, perm_ref):
    wide = 4 * LANES

    @pl.when(pl.program_id(0) == 0)
    def _():
        row, col = iota((wide, wide), 0), iota((wide, wide), 1)
        within = (row >> 4 & 7) * 4 + (row & 3)
        target = (row >> 2 & 3) * LANES + (row >> 7) * GROUP + within
        perm_ref[...] = jnp.where(col == target, 1.0, 0.0).astype(jnp.bfloat16)

    for g in range(groups):
        lanes = pl.ds(g * LANES, LANES)
        parts = [x_ref[p, r, 0, :, lanes] for p in range(2) for r in range(2)]
        out = dot(jnp.concatenate(parts, axis=1), perm_ref[...]).astype(jnp.bfloat16)
        for q in range(QUADS):
            o_ref[g * QUADS + q] = out[:, q * LANES : (q + 1) * LANES]


def pack(capture, groups=4):
    rows, channels = capture.shape[3:]
    chans = channels // LANES
    return pl.pallas_call(
        functools.partial(pack_kernel, groups),
        out_shape=jax.ShapeDtypeStruct((chans * QUADS, rows, LANES), jnp.bfloat16),
        grid=(chans // groups,),
        in_specs=[pl.BlockSpec((2, 2, 1, rows, groups * LANES), lambda g: (0, 0, 0, 0, g))],
        out_specs=pl.BlockSpec((groups * QUADS, rows, LANES), lambda g: (g, 0, 0)),
        scratch_shapes=[VMEM((4 * LANES, 4 * LANES), jnp.bfloat16)],
        name="pack",
    )(capture)


PITCH = 64


def detect_kernel(
    slabs, unroll, rx, halo, fwd, inv, last, tw_c, tw_s, ch_c, ch_s, o_ref, a_re, a_im, b_re, b_im
):
    sources, _, rows, _ = rx.shape
    wide = 2 * LANES
    row, col = iota((wide, wide), 0), iota((wide, wide), 1)
    target = (row >> 5 & 1) * LANES + (row >> 6 & 1) * 64 + (row >> 7) * GROUP + (row & 31)
    perm = jnp.where(col == target, 1.0, 0.0).astype(jnp.bfloat16)
    span = sources * rows
    tail = span - NTAP

    def unpack(pieces, start, size):
        both = dot(jnp.concatenate(pieces, axis=1), perm)
        a_re[pl.ds(start, size), :] = both[:, :LANES]
        a_im[pl.ds(start, size), :] = both[:, LANES:]

    for src in range(sources):
        unpack([rx[src, s] for s in slabs], NTAP + src * rows, rows)
        low = max(tail, src * rows)
        size = (src + 1) * rows - low
        if size > 0:
            pieces = []
            for s in slabs:
                if s == 0:
                    pieces.append(halo[low - tail : low - tail + size])
                else:
                    pieces.append(rx[src, s - 1, low - src * rows :])
            unpack(pieces, low - tail, size)

    def column(re, im, i):
        at = pl.ds(i, RADIX, stride=RADIX)
        return jnp.concatenate([re[at, :], im[at, :]], axis=0).astype(jnp.bfloat16)

    def block(re, im, i):
        at = pl.ds(pl.multiple_of(i * RADIX, RADIX), RADIX)
        return jnp.concatenate([re[at, :], im[at, :]], axis=0).astype(jnp.bfloat16)

    def split(out):
        half = out.shape[0] // 2
        return out[:half], out[half:]

    def at_of(i):
        return pl.ds(pl.multiple_of(i * RADIX, RADIX), RADIX)

    def first_stage(step, carry):
        for j in range(unroll):
            i = step * unroll + j
            re, im = split(dot(fwd[...], column(a_re, a_im, i)))
            cos, sin = tw_c[at_of(i), :], tw_s[at_of(i), :]
            b_re[at_of(i), :] = re * cos + im * sin
            b_im[at_of(i), :] = im * cos - re * sin
        return carry

    lax.fori_loop(0, RADIX // unroll, first_stage, 0)

    def middle_stages(step, carry):
        for j in range(unroll):
            i = step * unroll + j
            re, im = split(dot(fwd[...], column(b_re, b_im, i)))
            cos, sin = ch_c[at_of(i), :], ch_s[at_of(i), :]
            filtered = jnp.concatenate([re * cos + im * sin, im * cos - re * sin], axis=0)
            re, im = split(dot(inv[...], filtered.astype(jnp.bfloat16)))
            cos, sin = tw_c[at_of(i), :], tw_s[at_of(i), :]
            a_re[at_of(i), :] = re * cos - im * sin
            a_im[at_of(i), :] = im * cos + re * sin
        return carry

    lax.fori_loop(0, RADIX // unroll, middle_stages, 0)

    kept = last.shape[0] // 2

    def last_stage(step, carry):
        for j in range(unroll):
            i = step * unroll + j
            re, im = split(dot(last[...], column(a_re, a_im, i)) * (1.0 / NFFT))
            power = re * re + im * im
            power = power + pltpu.roll(power, 64, 1)
            o_ref[pl.ds(pl.multiple_of(i * kept, 16), kept), :] = power.astype(jnp.bfloat16)
        return carry

    lax.fori_loop(0, RADIX // unroll, last_stage, 0)


def detect(slabs, received, halo, tables, unroll=4):
    sources, _, rows, _ = received.shape
    span = sources * rows
    whole = pl.BlockSpec(memory_space=VMEM)
    args = [received, halo, *tables]
    flops = 2 * 2 * RADIX * 4 * 2 * RADIX * RADIX * LANES
    scratch = [VMEM((NFFT, LANES), jnp.float32)] * 4
    return pl.pallas_call(
        functools.partial(detect_kernel, slabs, unroll),
        out_shape=jax.ShapeDtypeStruct((span, LANES), jnp.bfloat16),
        in_specs=[whole] * len(args),
        out_specs=whole,
        scratch_shapes=scratch,
        cost_estimate=pl.CostEstimate(flops=flops, bytes_accessed=16 << 20, transcendentals=0),
        name="detect",
    )(*args)


def fold_kernel(late, early, keys, onehot, o_ref, turned):
    span = late.shape[0]
    chunk = 512
    lane = iota((LANES, LANES), 1)
    for t in range(span // LANES):
        at = pl.ds(t * LANES, LANES)
        both = jnp.where(lane < 64, early[at, :].astype(jnp.float32), late[at, :].astype(jnp.float32))
        turned[:, at] = both.T
    total = jnp.zeros((KEYS * GROUP, PAGE), jnp.float32)
    for q in range(QUADS):
        for t in range(span // chunk):
            at = pl.ds(t * chunk, chunk)
            own = turned[q * GROUP : (q + 1) * GROUP, at]
            key = jnp.broadcast_to(keys[q : q + 1, at], own.shape)
            picked = [jnp.where(key == u, own, 0.0).astype(jnp.bfloat16) for u in range(KEYS)]
            total = total + dot(jnp.concatenate(picked, axis=0), onehot[q, at, :])
    o_ref[...] = total.astype(jnp.bfloat16)


def fold(late, early, keys, onehot):
    whole = pl.BlockSpec(memory_space=VMEM)
    span = late.shape[0]
    flops = 2 * KEYS * GROUP * PAGE * QUADS * span
    return pl.pallas_call(
        fold_kernel,
        out_shape=jax.ShapeDtypeStruct((KEYS * GROUP, PAGE), jnp.bfloat16),
        in_specs=[whole] * 4,
        out_specs=whole,
        scratch_shapes=[VMEM((LANES, span), jnp.float32)],
        cost_estimate=pl.CostEstimate(flops=flops, bytes_accessed=8 << 20, transcendentals=0),
        name="fold",
    )(late, early, keys, onehot)


def swapped(x, axis):
    other = lax.ppermute(x, axis, [(0, 1), (1, 0)])
    low = lax.axis_index(axis) == 0
    return jnp.concatenate([jnp.where(low, x, other), jnp.where(low, other, x)], axis=0)


def shards(capture, chirp_rates, phase_bin, sub_id):
    rows = capture.shape[3]
    packed = pack(capture)
    received = lax.all_to_all(packed, ("chan", "zl", "xh"), 0, 0, tiled=True)
    received = received.reshape(-1, QUADS, rows, LANES)

    span = phase_bin.shape[0]
    keys = swapped(swapped((sub_id * BINS + phase_bin)[None], "xh"), "zl")
    keys = keys.reshape(QUADS, span // RADIX, RADIX).transpose(0, 2, 1).reshape(QUADS, span)
    own = lax.axis_index("zl") * 2 + lax.axis_index("xh")
    rates = lax.dynamic_index_in_dim(chirp_rates.reshape(-1, QUADS, 4), own, 1, False)
    rates = jnp.tile(rates.reshape(GROUP), LANES // GROUP)
    tables = (*transform_tables(), *chirp_table(rates))
    low = keys & (PAGE - 1)
    onehot = (low[:, :, None] == jnp.arange(PAGE, dtype=jnp.int32)).astype(jnp.bfloat16)

    tail = received[:, QUADS - 1].reshape(span, LANES)[span - NTAP :]
    blocks = lax.axis_size("zh")
    halo = lax.ppermute(tail, "zh", [(i, i + 1) for i in range(blocks - 1)])
    late = detect((2, 3), received, tail, tables)
    early = detect((0, 1), received, halo, tables)
    partial = fold(late, early, keys // PAGE, onehot)
    pieces = partial.reshape(KEYS, blocks, 4, PAGE).transpose(1, 0, 2, 3)
    pieces = lax.all_to_all(pieces.reshape(blocks, KEYS * 4, PAGE), "zh", 0, 0, tiled=True)
    scale = NSUB * BINS / (4.0 * span * blocks * QUADS)
    summed = jnp.sum(pieces.astype(jnp.float32), axis=0) * scale
    return summed.reshape(NSUB, BINS // PAGE, 4, PAGE).transpose(2, 0, 1, 3).reshape(4, NSUB, BINS)


def solution(mesh):
    chans, slabs = mesh.devices.shape
    fine = Mesh(mesh.devices.reshape(chans, slabs // QUADS, 2, 2), ("chan", "zh", "zl", "xh"))
    slab = ("zh", "zl", "xh")
    placed = (P(None, None, slab, "chan", None), P("chan"), P(slab), P(slab))
    return jax.shard_map(
        shards,
        mesh=fine,
        in_specs=placed,
        out_specs=P(("chan", *slab), None, None),
        check_vma=False,
    )
```

time: 184 us -> 158 us (0.86)
  the two profiles are of different devices: /device:TPU:6 before, /device:TPU:16 now
where the time goes in v2:
time: 158 us
  Pallas kernels  60.3 us (38%)
  blocking collectives  26.7 us (17%)
  starting transfers between devices  25 us (16%)
  waiting for transfers between devices  22 us (14%)
  other arithmetic  17.1 us (11%)
  local copies, waits for them, and re-layouts  6.46 us (4%)
    pallas_call x2, Pallas kernels, detect(): pl.pallas_call(functools.partial(detect_kernel, slabs, unroll), out_shape...  49 us
    all_to_all x1, blocking collectives, shards(): lax.all_to_all(pieces.reshape(blocks, KEYS * 4, PAGE), 'zh', 0, 0, tiled=...  26.7 us
    ppermute x2, waiting for transfers between devices, swapped(): other = lax.ppermute(x, axis, [(0, 1), (1, 0)])  22 us
    all_to_all x1, starting transfers between devices, shards(): received = lax.all_to_all(packed, ('chan', 'zl', 'xh'), 0, 0, tiled=True)  10.2 us
    ppermute x2, starting transfers between devices, swapped(): other = lax.ppermute(x, axis, [(0, 1), (1, 0)])  9.66 us
    sin x1, other arithmetic, chirp_table(): jnp.sin(phase).reshape(-1, LANES)  9.54 us
    pallas_call x1, Pallas kernels, fold(): pl.pallas_call(fold_kernel, out_shape=jax.ShapeDtypeStruct((KEYS * GROUP,...  5.8 us
    pallas_call x1, Pallas kernels, pack(): pl.pallas_call(functools.partial(pack_kernel, groups), out_shape=jax.Shap...  5.47 us
  transfers between devices with their start and end apart: 4, of which 2 were waited for; matrix products, arithmetic and copies ran while one was open for 14% of the time, Pallas kernels for 16%

profile of v2, /device:TPU:16, one launch (start us, length us, event | category | flops | bytes accessed | tf_op | source)
XLA Modules:
  0.0 157.7 jit_solution(2304470753879548900)
XLA Ops:
  0.0 5.5 %pack.1 = bf16[64,192,128]{2,1,0:T(8,128)(2,1)} custom-call(bf16[2,2,1,192,2048]{4,3,2,1,0:T(8,128)(2,1)} %x_ref.1), custom_call_target="tpu_custom_call" | custom-call | tf_op jit(solution)/shard_map/pack/pallas_call | solution.py:87
  5.5 10.2 %all-to-all-start = ((bf16[64,192,128]{2,1,0:T(8,128)(2,1)}), bf16[64,192,128]{2,1,0:T(8,128)(2,1)S(1)}, u32[]{:S(2)}, u32[]{:S(2)}) async-start(bf16[64,192,128]{2,1,0:T(8,128)(2,1)} %pack.1), calls=%async_computation | async-start | bytes 6291456 | tf_op jit(solution)/shard_map/all_to_all | solution.py:245
  15.7 4.9 %collective-permute-start.1 = (s32[1,3072]{1,0:T(1,128)S(1)}, s32[1,3072]{1,0:T(1,128)S(1)}, u32[]{:S(2)}, u32[]{:S(2)}) collective-permute-start(s32[1,3072]{1,0:T(1,128)S(1)} %bitcast.15), channel_id=1, source_target_pairs={{0,1},{1,0},{2,3},{3,2},{4,5},{5,4},{6,7},{7,6},{8,9},{9,8},{10,11... | collective-permute-start | bytes 36872 | tf_op jit(solution)/shard_map/ppermute | solution.py:237
  20.6 0.1 reshape.120
  20.8 0.1 tile.7
  20.9 0.1 mul.227
  21.0 0.1 add.88
  21.1 0.1 mul.220
  21.2 0.1 mul.222
  21.2 0.1 fusion.25
  21.4 0.2 sine_convert_fusion
  21.5 0.1 fusion.26
  21.6 9.5 %fusion.2 = (f32[4096,128]{1,0:T(8,128)}, f32[4096,128]{1,0:T(8,128)}) fusion(f32[4096]{0:T(1024)S(1)} %get-tuple-element.17, f32[128]{0:T(128)S(1)} %mul.227), kind=kLoop, calls=%fused_computation.4 | loop fusion | flops 2097152 | bytes 4211200 | tf_op jit(solution)/shard_map/sin | solution.py:55
  31.2 0.7 fusion.9
  31.9 20.9 %collective-permute-done.1 = s32[1,3072]{1,0:T(1,128)S(1)} collective-permute-done((s32[1,3072]{1,0:T(1,128)S(1)}, s32[1,3072]{1,0:T(1,128)S(1)}, u32[]{:S(2)}, u32[]{:S(2)}) %collective-permute-start.1) | collective-permute-done | bytes 12320 | tf_op jit(solution)/shard_map/ppermute | solution.py:237
  52.8 4.8 %collective-permute-start.2 = (s32[2,3072]{1,0:T(2,128)S(1)}, s32[2,3072]{1,0:T(2,128)S(1)}, u32[]{:S(2)}, u32[]{:S(2)}) collective-permute-start(s32[2,3072]{1,0:T(2,128)S(1)} %pad_add_fusion.1), channel_id=1, source_target_pairs={{0,2},{2,0},{1,3},{3,1},{4,6},{6,4},{5,7},{7,5},{8,10},{10,8},{9,1... | collective-permute-start | bytes 73736 | tf_op jit(solution)/shard_map/ppermute | solution.py:237
  57.6 0.7 fusion.17.last
  58.3 1.1 collective-permute-done.2
  59.5 0.1 reshape.121
  59.6 0.1 copy.10
  59.7 0.1 reshape.122
  59.8 0.7 broadcast_and_fusion
  60.6 5.1 %collective-permute-start = (bf16[1024,128]{1,0:T(8,128)(2,1)S(1)}, bf16[1024,128]{1,0:T(8,128)(2,1)}, u32[]{:S(2)}, u32[]{:S(2)}) collective-permute-start(bf16[1024,128]{1,0:T(8,128)(2,1)S(1)} %slice.17.halo), channel_id=1, source_target_pairs={{0,4},{4,8},{8,12},{12,16},{16,20},{20,24},{24,28},{1,5},{5,9},{9,... | collective-permute-start | bytes 786440 | tf_op jit(solution)/shard_map/ppermute | solution.py:260
  65.7 5.0 %fusion.onehot = bf16[4,3072,256]{2,1,0:T(8,128)(2,1)} fusion(s32[4,3072]{1,0:T(4,128)S(1)} %get-tuple-element.5), kind=kLoop, calls=%fused_computation.1 | loop fusion | flops 6291456 | bytes 6340608 | tf_op jit(solution)/shard_map/convert_element_type | solution.py:256
  70.7 1.9 %broadcast_in_dim.10.tw_c = f32[4096,128]{1,0:T(8,128)} broadcast(f32[4096]{0:T(1024)S(1)} %get-tuple-element.12), dimensions={0} | broadcast | bytes 2113536 | tf_op jit(solution)/shard_map/broadcast_in_dim | solution.py:44
  72.6 1.9 %broadcast_in_dim.11.tw_s = f32[4096,128]{1,0:T(8,128)} broadcast(f32[4096]{0:T(1024)S(1)} %get-tuple-element.11), dimensions={0} | broadcast | bytes 2113536 | tf_op jit(solution)/shard_map/broadcast_in_dim | solution.py:45
  74.5 24.5 %detect.2.late = bf16[3072,128]{1,0:T(8,128)(2,1)} custom-call(bf16[16,4,192,128]{3,2,1,0:T(8,128)(2,1)} %bitcast.9, bf16[1024,128]{1,0:T(8,128)(2,1)} %copy-done.1, bf16[128,128]{1,0:T(8,128)(2,1)} %get-tuple-element.10.fwd, bf16[128,128]{1,0:T(8,128)(2,1)} %get-tuple-element.9.inv, bf16[96,128]{1,0:T(8,128)(2,1)} %fusion.17.last, ...), custom_call_target="tpu_custom_call" | custom-call | flops 1073741824 | bytes 16777216 | tf_op jit(solution)/shard_map/detect/pallas_call | solution.py:191
  99.0 24.5 %detect.3.early = bf16[3072,128]{1,0:T(8,128)(2,1)} custom-call(bf16[16,4,192,128]{3,2,1,0:T(8,128)(2,1)} %bitcast.10, bf16[1024,128]{1,0:T(8,128)(2,1)} %collective-permute-done.halo, bf16[128,128]{1,0:T(8,128)(2,1)} %get-tuple-element.10.fwd, bf16[128,128]{1,0:T(8,128)(2,1)} %get-tuple-element.9.inv, bf16[96,128]{1,0:T(8,128)(2,1)} %fusion.17.last, ...), custom_call_target="tpu_custom_call" | custom-call | flops 1073741824 | bytes 16777216 | tf_op jit(solution)/shard_map/detect/pallas_call | solution.py:191
  123.5 5.8 %fold.1 = bf16[256,256]{1,0:T(8,128)(2,1)} custom-call(bf16[3072,128]{1,0:T(8,128)(2,1)} %detect.2.late, bf16[3072,128]{1,0:T(8,128)(2,1)} %detect.3.early, s32[4,3072]{1,0:T(4,128)} %get-tuple-element.6.keys, bf16[4,3072,256]{2,1,0:T(8,128)(2,1)} %fusion.onehot), custom_call_target="tpu_custom_call" | custom-call | flops 1610612736 | bytes 8388608 | tf_op jit(solution)/shard_map/fold/pallas_call | solution.py:225
  129.3 0.9 reshape.123
  130.3 26.7 %all_to_all.10 = bf16[8,32,256]{2,1,0:T(8,128)(2,1)S(1)} all-to-all(bf16[8,32,256]{2,1,0:T(8,128)(2,1)S(1)} %copy.12), channel_id=1, replica_groups=mesh['chan'=16,'zh'=8,'zl'=2,'xh'=2] {'zh'}, dimensions={0} | all-to-all | bytes 262144 | tf_op jit(solution)/shard_map/all_to_all | solution.py:265
  157.1 0.6 reshape.125
  (31 shorter events, 0.4 us)
Async XLA Ops:
  5.5 10.2 %copy-start.2 = (s32[3072]{0:T(1024)S(1)}, s32[3072]{0:T(1024)}, u32[]{:S(2)}) copy-start(s32[3072]{0:T(1024)} %param.6) | copy-start | bytes 36868
  5.5 10.2 %copy-start.3 = (s32[3072]{0:T(1024)S(1)}, s32[3072]{0:T(1024)}, u32[]{:S(2)}) copy-start(s32[3072]{0:T(1024)} %param.7) | copy-start | bytes 36868
  5.5 15.1 %copy-start.4 = (f32[128]{0:T(128)S(1)}, f32[128]{0:T(128)}, u32[]{:S(2)}) copy-start(f32[128]{0:T(128)} %param.5) | copy-start | bytes 1540
  5.5 55.0 %all-to-all-start = ((bf16[64,192,128]{2,1,0:T(8,128)(2,1)}), bf16[64,192,128]{2,1,0:T(8,128)(2,1)S(1)}, u32[]{:S(2)}, u32[]{:S(2)}) async-start(bf16[64,192,128]{2,1,0:T(8,128)(2,1)} %pack.1), calls=%async_computation | async-start | bytes 6291456 | tf_op jit(solution)/shard_map/all_to_all | solution.py:245
  15.7 37.0 %collective-permute-start.1 = (s32[1,3072]{1,0:T(1,128)S(1)}, s32[1,3072]{1,0:T(1,128)S(1)}, u32[]{:S(2)}, u32[]{:S(2)}) collective-permute-start(s32[1,3072]{1,0:T(1,128)S(1)} %bitcast.15), channel_id=1, source_target_pairs={{0,1},{1,0},{2,3},{3,2},{4,5},{5,4},{6,7},{7,6},{8,9},{9,8},{10,11... | collective-permute-start | bytes 36872 | tf_op jit(solution)/shard_map/ppermute | solution.py:237
  52.8 6.6 %collective-permute-start.2 = (s32[2,3072]{1,0:T(2,128)S(1)}, s32[2,3072]{1,0:T(2,128)S(1)}, u32[]{:S(2)}, u32[]{:S(2)}) collective-permute-start(s32[2,3072]{1,0:T(2,128)S(1)} %pad_add_fusion.1), channel_id=1, source_target_pairs={{0,2},{2,0},{1,3},{3,1},{4,6},{6,4},{5,7},{7,5},{8,10},{10,8},{9,1... | collective-permute-start | bytes 73736 | tf_op jit(solution)/shard_map/ppermute | solution.py:237
  60.5 10.2 %copy-start = (bf16[64,192,128]{2,1,0:T(8,128)(2,1)}, bf16[64,192,128]{2,1,0:T(8,128)(2,1)S(1)}, u32[]{:S(2)}) copy-start(bf16[64,192,128]{2,1,0:T(8,128)(2,1)S(1)} %all-to-all-done) | copy-start | bytes 9437188
  60.6 10.1 %copy-start.1 = (bf16[1024,128]{1,0:T(8,128)(2,1)}, bf16[1024,128]{1,0:T(8,128)(2,1)S(1)}, u32[]{:S(2)}) copy-start(bf16[1024,128]{1,0:T(8,128)(2,1)S(1)} %slice.17.halo) | copy-start | bytes 786436
  60.6 38.4 %collective-permute-start = (bf16[1024,128]{1,0:T(8,128)(2,1)S(1)}, bf16[1024,128]{1,0:T(8,128)(2,1)}, u32[]{:S(2)}, u32[]{:S(2)}) collective-permute-start(bf16[1024,128]{1,0:T(8,128)(2,1)S(1)} %slice.17.halo), channel_id=1, source_target_pairs={{0,4},{4,8},{8,12},{12,16},{16,20},{20,24},{24,28},{1,5},{5,9},{9,... | collective-permute-start | bytes 786440 | tf_op jit(solution)/shard_map/ppermute | solution.py:260

commit v3 on v2

v3 whole, which is shorter than its diff:
```python
import functools
import math

import jax
import jax.numpy as jnp
from jax import lax
from jax.experimental import pallas as pl
from jax.experimental.pallas import tpu as pltpu
from jax.sharding import Mesh
from jax.sharding import PartitionSpec as P

RADIX = 64
BINS = 1024
NSUB = 2
NFFT = 4096
NTAP = 1024
LANES = 128
GROUP = 32
QUADS = 4
PAGE = 256
KEYS = NSUB * BINS // PAGE
VMEM = pltpu.VMEM
GRANT = 16 << 20


def real_form(cosine, sine):
    top = jnp.concatenate([cosine, sine], axis=1)
    bottom = jnp.concatenate([-sine, cosine], axis=1)
    return jnp.concatenate([top, bottom], axis=0)


def transform_tables():
    indices = jnp.arange(RADIX, dtype=jnp.int32)
    small = indices[:, None] * indices[None, :] % RADIX
    angles = 2.0 * math.pi / RADIX * small.astype(jnp.float32)
    cosine = jnp.cos(angles).astype(jnp.bfloat16)
    sine = jnp.sin(angles).astype(jnp.bfloat16)
    forward = real_form(cosine, sine)
    inverse = real_form(cosine, -sine)
    first = NTAP // RADIX
    last = jnp.concatenate([inverse[first:RADIX], inverse[RADIX + first :]], axis=0)
    large = indices[:, None] * indices[None, :] % NFFT
    twist = 2.0 * math.pi / NFFT * large.astype(jnp.float32)
    row = jnp.arange(2 * LANES, dtype=jnp.int32)
    target = (row >> 5 & 1) * LANES + (row >> 6 & 1) * 64 + (row >> 7) * GROUP + (row & 31)
    perm = (target[:, None] == row[None, :]).astype(jnp.bfloat16)
    return (perm, forward, inverse, last), (jnp.cos(twist), jnp.sin(twist))


def chirp_table(rates_here):
    indices = jnp.arange(RADIX, dtype=jnp.int32)
    spectral = indices[:, None] + RADIX * indices[None, :]
    offset = ((spectral + NFFT // 2) % NFFT).astype(jnp.float32) / NFFT
    turns = rates_here[None, None, :] * (offset * offset)[:, :, None]
    phase = 2.0 * math.pi * (turns - jnp.floor(turns))
    return jnp.cos(phase).reshape(-1, LANES), jnp.sin(phase).reshape(-1, LANES)


def spread_kernel(tw_c, tw_s, ch_c, ch_s, otw_c, otw_s, och_c, och_s):
    for i in range(RADIX):
        at = pl.ds(i * RADIX, RADIX)
        otw_c[at, :] = jnp.broadcast_to(tw_c[:, i : i + 1], (RADIX, LANES))
        otw_s[at, :] = jnp.broadcast_to(tw_s[:, i : i + 1], (RADIX, LANES))
        och_c[at, :] = ch_c[at, :]
        och_s[at, :] = ch_s[at, :]


def all_tables(rates):
    matrices, twiddles = transform_tables()
    whole = pl.BlockSpec(memory_space=VMEM)
    spread = pl.pallas_call(
        spread_kernel,
        out_shape=[jax.ShapeDtypeStruct((NFFT, LANES), jnp.float32)] * 4,
        in_specs=[whole] * 4,
        out_specs=[whole] * 4,
        compiler_params=pltpu.CompilerParams(vmem_limit_bytes=GRANT),
        name="spread",
    )(*twiddles, *chirp_table(rates))
    return (*matrices, *spread)


def iota(shape, axis):
    return lax.broadcasted_iota(jnp.int32, shape, axis)


def dot(a, b):
    return jnp.dot(a, b, preferred_element_type=jnp.float32)


def pack_kernel(groups, x_ref, o_ref, perm_ref):
    wide = 4 * LANES

    @pl.when(pl.program_id(0) == 0)
    def _():
        row, col = iota((wide, wide), 0), iota((wide, wide), 1)
        within = (row >> 4 & 7) * 4 + (row & 3)
        target = (row >> 2 & 3) * LANES + (row >> 7) * GROUP + within
        perm_ref[...] = jnp.where(col == target, 1.0, 0.0).astype(jnp.bfloat16)

    for g in range(groups):
        lanes = pl.ds(g * LANES, LANES)
        parts = [x_ref[p, r, 0, :, lanes] for p in range(2) for r in range(2)]
        out = dot(jnp.concatenate(parts, axis=1), perm_ref[...]).astype(jnp.bfloat16)
        for q in range(QUADS):
            o_ref[g * QUADS + q] = out[:, q * LANES : (q + 1) * LANES]


def pack(capture, groups=4):
    rows, channels = capture.shape[3:]
    chans = channels // LANES
    return pl.pallas_call(
        functools.partial(pack_kernel, groups),
        out_shape=jax.ShapeDtypeStruct((chans * QUADS, rows, LANES), jnp.bfloat16),
        grid=(chans // groups,),
        in_specs=[pl.BlockSpec((2, 2, 1, rows, groups * LANES), lambda g: (0, 0, 0, 0, g))],
        out_specs=pl.BlockSpec((groups * QUADS, rows, LANES), lambda g: (g, 0, 0)),
        scratch_shapes=[VMEM((4 * LANES, 4 * LANES), jnp.bfloat16)],
        name="pack",
    )(capture)


PAIR = 2
PITCH = 68


def detect_kernel(
    slabs, unroll, rx, halo, perm, fwd, inv, last, tw_c, tw_s, ch_c, ch_s, o_ref, a_re, a_im, b_re, b_im
):
    sources, _, rows, _ = rx.shape
    span = sources * rows
    tail = span - NTAP

    def unpack(pieces, start, size):
        both = dot(jnp.concatenate(pieces, axis=1), perm[...])
        for j in range(size // RADIX):
            rows_at = pl.ds((start // RADIX + j) * PITCH, RADIX)
            part = both[j * RADIX : (j + 1) * RADIX]
            a_re[rows_at, :] = part[:, :LANES]
            a_im[rows_at, :] = part[:, LANES:]

    for src in range(sources):
        unpack([rx[src, s] for s in slabs], NTAP + src * rows, rows)
        low = max(tail, src * rows)
        size = (src + 1) * rows - low
        if size > 0:
            pieces = []
            for s in slabs:
                if s == 0:
                    pieces.append(halo[low - tail : low - tail + size])
                else:
                    pieces.append(rx[src, s - 1, low - src * rows :])
            unpack(pieces, low - tail, size)

    def column(re, im, i):
        at = pl.ds(i, RADIX, stride=PITCH)
        return jnp.concatenate([re[at, :], im[at, :]], axis=0).astype(jnp.bfloat16)

    def columns(re, im, i):
        return jnp.concatenate([column(re, im, i + j) for j in range(PAIR)], axis=1)

    def split(out, j):
        half = out.shape[0] // 2
        own = out[:, j * LANES : (j + 1) * LANES]
        return own[:half], own[half:]

    def at_of(i):
        return pl.ds(pl.multiple_of(i * RADIX, RADIX), RADIX)

    def pitched(i):
        return pl.ds(i * PITCH, RADIX)

    def loop(body):
        def many(step, carry):
            for j in range(unroll // PAIR):
                body(step * unroll + j * PAIR)
            return carry

        lax.fori_loop(0, RADIX // unroll, many, 0)

    def first_stage(i):
        out = dot(fwd[...], columns(a_re, a_im, i))
        for j in range(PAIR):
            re, im = split(out, j)
            cos, sin = tw_c[at_of(i + j), :], tw_s[at_of(i + j), :]
            b_re[pitched(i + j), :] = re * cos + im * sin
            b_im[pitched(i + j), :] = im * cos - re * sin

    loop(first_stage)

    def middle_stages(i):
        out = dot(fwd[...], columns(b_re, b_im, i))
        filtered = []
        for j in range(PAIR):
            re, im = split(out, j)
            cos, sin = ch_c[at_of(i + j), :], ch_s[at_of(i + j), :]
            both = jnp.concatenate([re * cos + im * sin, im * cos - re * sin], axis=0)
            filtered.append(both.astype(jnp.bfloat16))
        out = dot(inv[...], jnp.concatenate(filtered, axis=1))
        for j in range(PAIR):
            re, im = split(out, j)
            cos, sin = tw_c[at_of(i + j), :], tw_s[at_of(i + j), :]
            a_re[pitched(i + j), :] = re * cos - im * sin
            a_im[pitched(i + j), :] = im * cos + re * sin

    loop(middle_stages)

    kept = last.shape[0] // 2

    def last_stage(i):
        out = dot(last[...], columns(a_re, a_im, i)) * (1.0 / NFFT)
        for j in range(PAIR):
            re, im = split(out, j)
            power = re * re + im * im
            power = power + pltpu.roll(power, 64, 1)
            at = pl.ds(pl.multiple_of((i + j) * kept, 16), kept)
            o_ref[at, :] = power.astype(jnp.bfloat16)

    loop(last_stage)


def detect(slabs, received, halo, tables, unroll=32):
    sources, _, rows, _ = received.shape
    span = sources * rows
    whole = pl.BlockSpec(memory_space=VMEM)
    args = [received, halo, *tables]
    flops = 2 * 2 * RADIX * 4 * 2 * RADIX * RADIX * LANES
    scratch = [VMEM((RADIX * PITCH, LANES), jnp.float32)] * 4
    return pl.pallas_call(
        functools.partial(detect_kernel, slabs, unroll),
        out_shape=jax.ShapeDtypeStruct((span, LANES), jnp.bfloat16),
        in_specs=[whole] * len(args),
        out_specs=whole,
        scratch_shapes=scratch,
        cost_estimate=pl.CostEstimate(flops=flops, bytes_accessed=16 << 20, transcendentals=0),
        compiler_params=pltpu.CompilerParams(vmem_limit_bytes=GRANT),
        name="detect",
    )(*args)


def fold_kernel(late, early, keys, o_ref, turned):
    span = late.shape[0]
    chunk = 512
    lane = iota((LANES, LANES), 1)
    for t in range(span // LANES):
        at = pl.ds(t * LANES, LANES)
        both = jnp.where(lane < 64, early[at, :].astype(jnp.float32), late[at, :].astype(jnp.float32))
        turned[:, at] = both.T
    total = jnp.zeros((KEYS * GROUP, PAGE), jnp.float32)
    for q in range(QUADS):
        for t in range(span // chunk):
            at = pl.ds(t * chunk, chunk)
            code = keys[q : q + 1, at]
            shape = (KEYS, chunk)
            mine = jnp.broadcast_to(code >> 8, shape) == iota(shape, 0)
            picked = []
            for c in range(q * GROUP, (q + 1) * GROUP):
                own = jnp.broadcast_to(turned[c : c + 1, at], shape)
                picked.append(jnp.where(mine, own, 0.0))
            picked = jnp.concatenate(picked, axis=0).astype(jnp.bfloat16)
            low = jnp.broadcast_to(code & (PAGE - 1), (PAGE, chunk))
            onehot = jnp.where(low == iota((PAGE, chunk), 0), 1.0, 0.0).astype(jnp.bfloat16)
            total = total + lax.dot_general(
                picked,
                onehot,
                (((1,), (1,)), ((), ())),
                preferred_element_type=jnp.float32,
            )
    o_ref[...] = total.astype(jnp.bfloat16)


def fold(late, early, keys):
    whole = pl.BlockSpec(memory_space=VMEM)
    span = late.shape[0]
    flops = 2 * KEYS * GROUP * PAGE * QUADS * span
    return pl.pallas_call(
        fold_kernel,
        out_shape=jax.ShapeDtypeStruct((KEYS * GROUP, PAGE), jnp.bfloat16),
        in_specs=[whole] * 3,
        out_specs=whole,
        scratch_shapes=[VMEM((LANES, span), jnp.float32)],
        cost_estimate=pl.CostEstimate(flops=flops, bytes_accessed=8 << 20, transcendentals=0),
        compiler_params=pltpu.CompilerParams(vmem_limit_bytes=GRANT),
        name="fold",
    )(late, early, keys)


def shared(mine):
    across = [(0, 1), (1, 0)]
    both = [(0, 3), (1, 2), (2, 1), (3, 0)]
    by_x = lax.ppermute(mine, "xh", across)
    by_z = lax.ppermute(mine, "zl", across)
    by_both = lax.ppermute(mine, ("zl", "xh"), both)
    x_low, z_low = lax.axis_index("xh") == 0, lax.axis_index("zl") == 0
    near = jnp.concatenate([jnp.where(x_low, mine, by_x), jnp.where(x_low, by_x, mine)])
    far = jnp.concatenate([jnp.where(x_low, by_z, by_both), jnp.where(x_low, by_both, by_z)])
    return jnp.concatenate([jnp.where(z_low, near, far), jnp.where(z_low, far, near)])


def shards(capture, chirp_rates, phase_bin, sub_id):
    rows = capture.shape[3]
    packed = pack(capture)
    received = lax.all_to_all(packed, ("chan", "zl", "xh"), 0, 0, tiled=True)
    received = received.reshape(-1, QUADS, rows, LANES)

    span = phase_bin.shape[0]
    mine = (sub_id * BINS + phase_bin).reshape(span // RADIX, RADIX).T.reshape(1, span)
    keys = shared(mine)
    own = lax.axis_index("zl") * 2 + lax.axis_index("xh")
    rates = lax.dynamic_index_in_dim(chirp_rates.reshape(-1, QUADS, 4), own, 1, False)
    rates = jnp.tile(rates.reshape(GROUP), LANES // GROUP)
    tables = all_tables(rates)
    first = (span - NTAP) // rows
    tail = received[first:, QUADS - 1].reshape(-1, LANES)[-NTAP:]
    ready = jnp.maximum(tables[4][0, 0], tables[6][0, 0]) < 2.0
    tail = jnp.where(ready, tail, jnp.zeros_like(tail))
    blocks = lax.axis_size("zh")
    halo = lax.ppermute(tail, "zh", [(i, i + 1) for i in range(blocks - 1)])
    late = detect((2, 3), received, tail, tables)
    early = detect((0, 1), received, halo, tables)
    partial = fold(late, early, keys)
    pieces = partial.reshape(blocks, 4 * KEYS, PAGE)
    pieces = lax.all_to_all(pieces, "zh", 0, 0, tiled=True)
    scale = NSUB * BINS / (4.0 * span * blocks * QUADS)
    summed = jnp.sum(pieces.astype(jnp.float32), axis=0) * scale
    return summed.reshape(4, NSUB, BINS)


def solution(mesh):
    chans, slabs = mesh.devices.shape
    fine = Mesh(mesh.devices.reshape(chans, slabs // QUADS, 2, 2), ("chan", "zh", "zl", "xh"))
    slab = ("zh", "zl", "xh")
    placed = (P(None, None, slab, "chan", None), P("chan"), P(slab), P(slab))
    return jax.shard_map(
        shards,
        mesh=fine,
        in_specs=placed,
        out_specs=P(("chan", *slab), None, None),
        check_vma=False,
    )
```

time: 158 us -> 111 us (0.70)
  the two profiles are of different devices: /device:TPU:16 before, /device:TPU:8 now
where the time goes in v3:
time: 111 us; the launch traced here: 110 us
  blocking collectives  32.7 us (29%)
  starting transfers between devices  25.5 us (23%)
  Pallas kernels  17.8 us (16%)
  local copies, waits for them, and re-layouts  17.4 us (16%)
  other arithmetic  10.5 us (9%)
  waiting for transfers between devices  4.87 us (4%)
  between operations  1.5 us (1%)
    all_to_all x1, blocking collectives, shards(): pieces = lax.all_to_all(pieces, 'zh', 0, 0, tiled=True)  32.7 us
    unnamed x26, local copies, waits for them, and re-layouts  15 us
    all_to_all x1, starting transfers between devices, shards(): received = lax.all_to_all(packed, ('chan', 'zl', 'xh'), 0, 0, tiled=True)  10.2 us
    sin x1, other arithmetic, chirp_table(): jnp.sin(phase).reshape(-1, LANES)  9.54 us
    pallas_call x2, Pallas kernels, detect(): pl.pallas_call(functools.partial(detect_kernel, slabs, unroll), out_shape...  8.94 us
    pallas_call x1, Pallas kernels, pack(): pl.pallas_call(functools.partial(pack_kernel, groups), out_shape=jax.Shap...  5.46 us
    ppermute x1, starting transfers between devices, shared(): by_both = lax.ppermute(mine, ('zl', 'xh'), both)  4.87 us
    ppermute x1, starting transfers between devices, shards(): halo = lax.ppermute(tail, 'zh', [(i, i + 1) for i in range(blocks - 1)])  4.58 us
  transfers between devices with their start and end apart: 5, of which 2 were waited for; matrix products, arithmetic and copies ran while one was open for 11% of the time, Pallas kernels for 5%

profile of v3, /device:TPU:8, one launch (start us, length us, event | category | flops | bytes accessed | tf_op | source)
XLA Modules:
  0.0 110.2 jit_solution(8446292647260196701)
XLA Ops:
  0.0 5.5 %pack.1 = bf16[64,192,128]{2,1,0:T(8,128)(2,1)} custom-call(bf16[2,2,1,192,2048]{4,3,2,1,0:T(8,128)(2,1)} %x_ref.1), custom_call_target="tpu_custom_call" | custom-call | tf_op jit(solution)/shard_map/pack/pallas_call | solution.py:111
  5.5 10.2 %all-to-all-start = ((bf16[64,192,128]{2,1,0:T(8,128)(2,1)}), bf16[64,192,128]{2,1,0:T(8,128)(2,1)S(1)}, u32[]{:S(2)}, u32[]{:S(2)}) async-start(bf16[64,192,128]{2,1,0:T(8,128)(2,1)} %pack.1), calls=%async_computation | async-start | bytes 6291456 | tf_op jit(solution)/shard_map/all_to_all | solution.py:302
  15.9 0.1 reshape.90
  16.0 3.4 %collective-permute-start.2 = (s32[1,3072]{1,0:T(1,128)S(1)}, s32[1,3072]{1,0:T(1,128)S(1)}, u32[]{:S(2)}, u32[]{:S(2)}) collective-permute-start(s32[1,3072]{1,0:T(1,128)S(1)} %reshape.90), channel_id=1, source_target_pairs={{0,2},{2,0},{1,3},{3,1},{4,6},{6,4},{5,7},{7,5},{8,10},{10,8},{9,1... | collective-permute-start | bytes 36872 | tf_op jit(solution)/shard_map/ppermute | solution.py:291
  19.4 4.9 %collective-permute-start.3 = (s32[1,3072]{1,0:T(1,128)S(1)}, s32[1,3072]{1,0:T(1,128)S(1)}, u32[]{:S(2)}, u32[]{:S(2)}) collective-permute-start(s32[1,3072]{1,0:T(1,128)S(1)} %reshape.90), channel_id=1, source_target_pairs={{0,3},{1,2},{2,1},{3,0},{4,7},{5,6},{6,5},{7,4},{8,11},{9,10},{10,... | collective-permute-start | bytes 36872 | tf_op jit(solution)/shard_map/ppermute | solution.py:292
  24.2 2.5 %collective-permute-start.1 = (s32[1,3072]{1,0:T(1,128)S(1)}, s32[1,3072]{1,0:T(1,128)S(1)}, u32[]{:S(2)}, u32[]{:S(2)}) collective-permute-start(s32[1,3072]{1,0:T(1,128)S(1)} %reshape.90), channel_id=1, source_target_pairs={{0,1},{1,0},{2,3},{3,2},{4,5},{5,4},{6,7},{7,6},{8,9},{9,8},{10,11... | collective-permute-start | bytes 36872 | tf_op jit(solution)/shard_map/ppermute | solution.py:290
  26.7 0.1 reshape.88
  27.3 0.1 fusion.27
  27.4 0.2 sine_convert_fusion
  27.6 0.1 fusion.25
  27.9 9.5 %fusion.1 = (f32[4096,128]{1,0:T(8,128)}, f32[4096,128]{1,0:T(8,128)}) fusion(f32[4096]{0:T(1024)S(1)} %fusion.24, f32[128]{0:T(128)S(1)} %mul.210), kind=kLoop, calls=%fused_computation.2 | loop fusion | flops 2097152 | bytes 4211200 | tf_op jit(solution)/shard_map/sin | solution.py:56
  37.6 1.6 %copy-done = f32[4096,128]{1,0:T(8,128)S(1)} copy-done((f32[4096,128]{1,0:T(8,128)S(1)}, f32[4096,128]{1,0:T(8,128)}, u32[]{:S(2)}) %copy-start) | copy-done | bytes 2097176
  39.2 1.6 %copy-done.1 = f32[4096,128]{1,0:T(8,128)S(1)} copy-done((f32[4096,128]{1,0:T(8,128)S(1)}, f32[4096,128]{1,0:T(8,128)}, u32[]{:S(2)}) %copy-start.1) | copy-done | bytes 2097176
  40.7 1.4 %spread.1 = (f32[4096,128]{1,0:T(8,128)S(1)}, f32[4096,128]{1,0:T(8,128)S(1)}, f32[4096,128]{1,0:T(8,128)S(1)}, f32[4096,128]{1,0:T(8,128)S(1)}) custom-call(f32[64,64]{1,0:T(8,128)S(1)} %get-tuple-element.24.tw_c, f32[64,64]{1,0:T(8,128)S(1)} %get-tuple-element.23.tw_s, f32[4096,128]{1,0:T(8,128)S(1)} %copy-done.1, f32[4096,128]{1,0:T(8,128)S(1)} %copy-done), custom_call_target="tpu_custom_call" | custom-call | tf_op jit(solution)/shard_map/spread/pallas_call | solution.py:71
  42.2 1.3 %copy-done.4 = f32[4096,128]{1,0:T(8,128)} copy-done((f32[4096,128]{1,0:T(8,128)}, f32[4096,128]{1,0:T(8,128)S(1)}, u32[]{:S(2)}) %copy-start.4) | copy-done | bytes 2097176
  43.5 1.4 %copy-done.8 = f32[4096,128]{1,0:T(8,128)} copy-done((f32[4096,128]{1,0:T(8,128)}, f32[4096,128]{1,0:T(8,128)S(1)}, u32[]{:S(2)}) %copy-start.8) | copy-done | bytes 2097176
  44.9 0.5 slice.18
  45.4 1.4 %copy-done.2 = f32[4096,128]{1,0:T(8,128)} copy-done((f32[4096,128]{1,0:T(8,128)}, f32[4096,128]{1,0:T(8,128)S(1)}, u32[]{:S(2)}) %copy-start.2) | copy-done | bytes 2097176
  46.8 0.5 slice.19
  47.3 1.3 %copy-done.6 = f32[4096,128]{1,0:T(8,128)} copy-done((f32[4096,128]{1,0:T(8,128)}, f32[4096,128]{1,0:T(8,128)S(1)}, u32[]{:S(2)}) %copy-start.6) | copy-done | bytes 2097176
  49.8 2.6 %collective-permute-done.1 = s32[1,3072]{1,0:T(1,128)S(1)} collective-permute-done((s32[1,3072]{1,0:T(1,128)S(1)}, s32[1,3072]{1,0:T(1,128)S(1)}, u32[]{:S(2)}, u32[]{:S(2)}) %collective-permute-start.1) | collective-permute-done | bytes 12320 | tf_op jit(solution)/shard_map/ppermute | solution.py:290
  52.5 2.2 %collective-permute-done.3 = s32[1,3072]{1,0:T(1,128)S(1)} collective-permute-done((s32[1,3072]{1,0:T(1,128)S(1)}, s32[1,3072]{1,0:T(1,128)S(1)}, u32[]{:S(2)}, u32[]{:S(2)}) %collective-permute-start.3) | collective-permute-done | bytes 12320 | tf_op jit(solution)/shard_map/ppermute | solution.py:292
  54.9 4.6 %collective-permute-start = (bf16[1024,128]{1,0:T(8,128)(2,1)S(1)}, bf16[1024,128]{1,0:T(8,128)(2,1)S(1)}, u32[]{:S(2)}, u32[]{:S(2)}) collective-permute-start(bf16[1024,128]{1,0:T(8,128)(2,1)S(1)} %slice_select_fusion.halo), channel_id=1, source_target_pairs={{0,4},{4,8},{8,12},{12,16},{16,20},{20,24},{24,28},{1,5},{5,9},{9,... | collective-permute-start | bytes 786440 | tf_op jit(solution)/shard_map/ppermute | solution.py:317
  59.5 1.6 %copy-done.3 = f32[4096,128]{1,0:T(8,128)S(1)} copy-done((f32[4096,128]{1,0:T(8,128)S(1)}, f32[4096,128]{1,0:T(8,128)}, u32[]{:S(2)}) %copy-start.3) | copy-done | bytes 2097176
  61.1 1.6 %copy-done.5 = f32[4096,128]{1,0:T(8,128)S(1)} copy-done((f32[4096,128]{1,0:T(8,128)S(1)}, f32[4096,128]{1,0:T(8,128)}, u32[]{:S(2)}) %copy-start.5) | copy-done | bytes 2097176
  62.7 1.6 %copy-done.7 = f32[4096,128]{1,0:T(8,128)S(1)} copy-done((f32[4096,128]{1,0:T(8,128)S(1)}, f32[4096,128]{1,0:T(8,128)}, u32[]{:S(2)}) %copy-start.7) | copy-done | bytes 2097176
  64.3 1.6 %copy-done.9 = f32[4096,128]{1,0:T(8,128)S(1)} copy-done((f32[4096,128]{1,0:T(8,128)S(1)}, f32[4096,128]{1,0:T(8,128)}, u32[]{:S(2)}) %copy-start.9) | copy-done | bytes 2097176
  65.9 4.5 %detect.2.late = bf16[3072,128]{1,0:T(8,128)(2,1)S(1)} custom-call(bf16[16,4,192,128]{3,2,1,0:T(8,128)(2,1)S(1)} %bitcast.6, bf16[1024,128]{1,0:T(8,128)(2,1)S(1)} %slice_select_fusion.halo, bf16[256,256]{1,0:T(8,128)(2,1)S(1)} %fusion.3.perm, bf16[128,128]{1,0:T(8,128)(2,1)S(1)} %get-tuple-element.16.fwd, bf16[128,128]{1,0:T(8,128)(2,1)S(1)} %get-tuple-element.15.inv, ...), custom_call_target="tpu_custom_call" | custom-call | flops 1073741824 | bytes 16777216 | tf_op jit(solution)/shard_map/detect/pallas_call | solution.py:228
  70.3 4.5 %detect.3.early = bf16[3072,128]{1,0:T(8,128)(2,1)S(1)} custom-call(bf16[16,4,192,128]{3,2,1,0:T(8,128)(2,1)S(1)} %bitcast.7, bf16[1024,128]{1,0:T(8,128)(2,1)S(1)} %collective-permute-done.halo, bf16[256,256]{1,0:T(8,128)(2,1)S(1)} %fusion.3.perm, bf16[128,128]{1,0:T(8,128)(2,1)S(1)} %get-tuple-element.16.fwd, bf16[128,128]{1,0:T(8,128)(2,1)S(1)} %get-tuple-element.15.inv, ...), custom_call_target="tpu_custom_call" | custom-call | flops 1073741824 | bytes 16777216 | tf_op jit(solution)/shard_map/detect/pallas_call | solution.py:228
  74.8 2.0 %fold.1 = bf16[256,256]{1,0:T(8,128)(2,1)S(1)} custom-call(bf16[3072,128]{1,0:T(8,128)(2,1)S(1)} %detect.2.late, bf16[3072,128]{1,0:T(8,128)(2,1)S(1)} %detect.3.early, s32[4,3072]{1,0:T(4,128)S(1)} %pad_add_fusion.keys), custom_call_target="tpu_custom_call" | custom-call | flops 1610612736 | bytes 8388608 | tf_op jit(solution)/shard_map/fold/pallas_call | solution.py:275
  76.8 32.7 %all_to_all.10 = bf16[8,32,256]{2,1,0:T(8,128)(2,1)S(1)} all-to-all(bf16[8,32,256]{2,1,0:T(8,128)(2,1)S(1)} %bitcast.8), channel_id=1, replica_groups=mesh['chan'=16,'zh'=8,'zl'=2,'xh'=2] {'zh'}, dimensions={0} | all-to-all | bytes 262144 | tf_op jit(solution)/shard_map/all_to_all | solution.py:322
  109.5 0.6 mul.233
  (44 shorter events, 1.1 us)
Async XLA Ops:
  5.5 10.2 %copy-start.10 = (s32[3072]{0:T(1024)S(1)}, s32[3072]{0:T(1024)}, u32[]{:S(2)}) copy-start(s32[3072]{0:T(1024)} %param.6) | copy-start | bytes 36868
  5.5 10.2 %copy-start.11 = (s32[3072]{0:T(1024)S(1)}, s32[3072]{0:T(1024)}, u32[]{:S(2)}) copy-start(s32[3072]{0:T(1024)} %param.7) | copy-start | bytes 36868
  5.5 21.3 %copy-start.12 = (f32[128]{0:T(128)S(1)}, f32[128]{0:T(128)}, u32[]{:S(2)}) copy-start(f32[128]{0:T(128)} %param.5) | copy-start | bytes 1540
  5.5 49.3 %all-to-all-start = ((bf16[64,192,128]{2,1,0:T(8,128)(2,1)}), bf16[64,192,128]{2,1,0:T(8,128)(2,1)S(1)}, u32[]{:S(2)}, u32[]{:S(2)}) async-start(bf16[64,192,128]{2,1,0:T(8,128)(2,1)} %pack.1), calls=%async_computation | async-start | bytes 6291456 | tf_op jit(solution)/shard_map/all_to_all | solution.py:302
  16.0 36.5 %collective-permute-start.2 = (s32[1,3072]{1,0:T(1,128)S(1)}, s32[1,3072]{1,0:T(1,128)S(1)}, u32[]{:S(2)}, u32[]{:S(2)}) collective-permute-start(s32[1,3072]{1,0:T(1,128)S(1)} %reshape.90), channel_id=1, source_target_pairs={{0,2},{2,0},{1,3},{3,1},{4,6},{6,4},{5,7},{7,5},{8,10},{10,8},{9,1... | collective-permute-start | bytes 36872 | tf_op jit(solution)/shard_map/ppermute | solution.py:291
  19.4 35.4 %collective-permute-start.3 = (s32[1,3072]{1,0:T(1,128)S(1)}, s32[1,3072]{1,0:T(1,128)S(1)}, u32[]{:S(2)}, u32[]{:S(2)}) collective-permute-start(s32[1,3072]{1,0:T(1,128)S(1)} %reshape.90), channel_id=1, source_target_pairs={{0,3},{1,2},{2,1},{3,0},{4,7},{5,6},{6,5},{7,4},{8,11},{9,10},{10,... | collective-permute-start | bytes 36872 | tf_op jit(solution)/shard_map/ppermute | solution.py:292
  24.2 28.2 %collective-permute-start.1 = (s32[1,3072]{1,0:T(1,128)S(1)}, s32[1,3072]{1,0:T(1,128)S(1)}, u32[]{:S(2)}, u32[]{:S(2)}) collective-permute-start(s32[1,3072]{1,0:T(1,128)S(1)} %reshape.90), channel_id=1, source_target_pairs={{0,1},{1,0},{2,3},{3,2},{4,5},{5,4},{6,7},{7,6},{8,9},{9,8},{10,11... | collective-permute-start | bytes 36872 | tf_op jit(solution)/shard_map/ppermute | solution.py:290
  37.6 1.6 %copy-start = (f32[4096,128]{1,0:T(8,128)S(1)}, f32[4096,128]{1,0:T(8,128)}, u32[]{:S(2)}) copy-start(f32[4096,128]{1,0:T(8,128)} %get-tuple-element.21.ch_s) | copy-start | bytes 6291460
  39.2 1.6 %copy-start.1 = (f32[4096,128]{1,0:T(8,128)S(1)}, f32[4096,128]{1,0:T(8,128)}, u32[]{:S(2)}) copy-start(f32[4096,128]{1,0:T(8,128)} %get-tuple-element.22.ch_c) | copy-start | bytes 6291460
  42.2 1.4 %copy-start.4 = (f32[4096,128]{1,0:T(8,128)}, f32[4096,128]{1,0:T(8,128)S(1)}, u32[]{:S(2)}) copy-start(f32[4096,128]{1,0:T(8,128)S(1)} %get-tuple-element.11.tw_s) | copy-start | bytes 6291460
  43.5 1.4 %copy-start.8 = (f32[4096,128]{1,0:T(8,128)}, f32[4096,128]{1,0:T(8,128)S(1)}, u32[]{:S(2)}) copy-start(f32[4096,128]{1,0:T(8,128)S(1)} %get-tuple-element.12.ch_s) | copy-start | bytes 6291460
  45.4 1.4 %copy-start.2 = (f32[4096,128]{1,0:T(8,128)}, f32[4096,128]{1,0:T(8,128)S(1)}, u32[]{:S(2)}) copy-start(f32[4096,128]{1,0:T(8,128)S(1)} %get-tuple-element.9.tw_c) | copy-start | bytes 6291460
  47.3 1.3 %copy-start.6 = (f32[4096,128]{1,0:T(8,128)}, f32[4096,128]{1,0:T(8,128)S(1)}, u32[]{:S(2)}) copy-start(f32[4096,128]{1,0:T(8,128)S(1)} %get-tuple-element.10.ch_c) | copy-start | bytes 6291460
  54.9 15.5 %collective-permute-start = (bf16[1024,128]{1,0:T(8,128)(2,1)S(1)}, bf16[1024,128]{1,0:T(8,128)(2,1)S(1)}, u32[]{:S(2)}, u32[]{:S(2)}) collective-permute-start(bf16[1024,128]{1,0:T(8,128)(2,1)S(1)} %slice_select_fusion.halo), channel_id=1, source_target_pairs={{0,4},{4,8},{8,12},{12,16},{16,20},{20,24},{24,28},{1,5},{5,9},{9,... | collective-permute-start | bytes 786440 | tf_op jit(solution)/shard_map/ppermute | solution.py:317
  59.5 1.6 %copy-start.3 = (f32[4096,128]{1,0:T(8,128)S(1)}, f32[4096,128]{1,0:T(8,128)}, u32[]{:S(2)}) copy-start(f32[4096,128]{1,0:T(8,128)} %copy-done.2) | copy-start | bytes 6291460
  61.1 1.6 %copy-start.5 = (f32[4096,128]{1,0:T(8,128)S(1)}, f32[4096,128]{1,0:T(8,128)}, u32[]{:S(2)}) copy-start(f32[4096,128]{1,0:T(8,128)} %copy-done.4) | copy-start | bytes 6291460
  62.7 1.6 %copy-start.7 = (f32[4096,128]{1,0:T(8,128)S(1)}, f32[4096,128]{1,0:T(8,128)}, u32[]{:S(2)}) copy-start(f32[4096,128]{1,0:T(8,128)} %copy-done.6) | copy-start | bytes 6291460
  64.3 1.6 %copy-start.9 = (f32[4096,128]{1,0:T(8,128)S(1)}, f32[4096,128]{1,0:T(8,128)}, u32[]{:S(2)}) copy-start(f32[4096,128]{1,0:T(8,128)} %copy-done.8) | copy-start | bytes 6291460

commit v4 on v3

--- a/solution.py
+++ b/solution.py
@@ -20,7 +20,8 @@
 PAGE = 256
 KEYS = NSUB * BINS // PAGE
 VMEM = pltpu.VMEM
-GRANT = 16 << 20
+GRANT = 24 << 20
+UNROLL = 32
 
 
 def real_form(cosine, sine):
@@ -41,10 +42,9 @@
     last = jnp.concatenate([inverse[first:RADIX], inverse[RADIX + first :]], axis=0)
     large = indices[:, None] * indices[None, :] % NFFT
     twist = 2.0 * math.pi / NFFT * large.astype(jnp.float32)
-    row = jnp.arange(2 * LANES, dtype=jnp.int32)
-    target = (row >> 5 & 1) * LANES + (row >> 6 & 1) * 64 + (row >> 7) * GROUP + (row & 31)
-    perm = (target[:, None] == row[None, :]).astype(jnp.bfloat16)
-    return (perm, forward, inverse, last), (jnp.cos(twist), jnp.sin(twist))
+    shape = (RADIX, RADIX // UNROLL, UNROLL)
+    twiddles = [w.reshape(shape).transpose(1, 0, 2) for w in (jnp.cos(twist), jnp.sin(twist))]
+    return forward, inverse, last, *twiddles
 
 
 def chirp_table(rates_here):
@@ -56,29 +56,6 @@
     return jnp.cos(phase).reshape(-1, LANES), jnp.sin(phase).reshape(-1, LANES)
 
 
-def spread_kernel(tw_c, tw_s, ch_c, ch_s, otw_c, otw_s, och_c, och_s):
-    for i in range(RADIX):
-        at = pl.ds(i * RADIX, RADIX)
-        otw_c[at, :] = jnp.broadcast_to(tw_c[:, i : i + 1], (RADIX, LANES))
-        otw_s[at, :] = jnp.broadcast_to(tw_s[:, i : i + 1], (RADIX, LANES))
-        och_c[at, :] = ch_c[at, :]
-        och_s[at, :] = ch_s[at, :]
-
-
-def all_tables(rates):
-    matrices, twiddles = transform_tables()
-    whole = pl.BlockSpec(memory_space=VMEM)
-    spread = pl.pallas_call(
-        spread_kernel,
-        out_shape=[jax.ShapeDtypeStruct((NFFT, LANES), jnp.float32)] * 4,
-        in_specs=[whole] * 4,
-        out_specs=[whole] * 4,
-        compiler_params=pltpu.CompilerParams(vmem_limit_bytes=GRANT),
-        name="spread",
-    )(*twiddles, *chirp_table(rates))
-    return (*matrices, *spread)
-
-
 def iota(shape, axis):
     return lax.broadcasted_iota(jnp.int32, shape, axis)
 
@@ -87,22 +64,24 @@
     return jnp.dot(a, b, preferred_element_type=jnp.float32)
 
 
-def pack_kernel(groups, x_ref, o_ref, perm_ref):
-    wide = 4 * LANES
-
-    @pl.when(pl.program_id(0) == 0)
-    def _():
-        row, col = iota((wide, wide), 0), iota((wide, wide), 1)
-        within = (row >> 4 & 7) * 4 + (row & 3)
-        target = (row >> 2 & 3) * LANES + (row >> 7) * GROUP + within
-        perm_ref[...] = jnp.where(col == target, 1.0, 0.0).astype(jnp.bfloat16)
-
+def pack_kernel(groups, x_ref, o_ref):
+    shape = (x_ref.shape[3], LANES)
+    lane = iota(shape, 1)
     for g in range(groups):
         lanes = pl.ds(g * LANES, LANES)
         parts = [x_ref[p, r, 0, :, lanes] for p in range(2) for r in range(2)]
-        out = dot(jnp.concatenate(parts, axis=1), perm_ref[...]).astype(jnp.bfloat16)
+        for bit in range(2):
+            step = 4 << bit
+            low = (lane & step) == 0
+            for s in range(4):
+                if s & (1 << bit) == 0:
+                    t = s | (1 << bit)
+                    parts[s], parts[t] = (
+                        jnp.where(low, parts[s], pltpu.roll(parts[t], step, 1)),
+                        jnp.where(low, pltpu.roll(parts[s], LANES - step, 1), parts[t]),
+                    )
         for q in range(QUADS):
-            o_ref[g * QUADS + q] = out[:, q * LANES : (q + 1) * LANES]
+            o_ref[g * QUADS + q] = parts[q]
 
 
 def pack(capture, groups=4):
@@ -114,7 +93,6 @@
         grid=(chans // groups,),
         in_specs=[pl.BlockSpec((2, 2, 1, rows, groups * LANES), lambda g: (0, 0, 0, 0, g))],
         out_specs=pl.BlockSpec((groups * QUADS, rows, LANES), lambda g: (g, 0, 0)),
-        scratch_shapes=[VMEM((4 * LANES, 4 * LANES), jnp.bfloat16)],
         name="pack",
     )(capture)
 
@@ -124,19 +102,28 @@
 
 
 def detect_kernel(
-    slabs, unroll, rx, halo, perm, fwd, inv, last, tw_c, tw_s, ch_c, ch_s, o_ref, a_re, a_im, b_re, b_im
+    slabs, rx, halo, fwd, inv, last, tw_c, tw_s, ch_c, ch_s, o_ref, a_re, a_im, b_re, b_im, c_c, c_s, sem
 ):
+    chirps = [
+        pltpu.make_async_copy(ch_c, c_c, sem.at[0]),
+        pltpu.make_async_copy(ch_s, c_s, sem.at[1]),
+    ]
+    for copy in chirps:
+        copy.start()
+    unroll = UNROLL
     sources, _, rows, _ = rx.shape
     span = sources * rows
     tail = span - NTAP
 
     def unpack(pieces, start, size):
-        both = dot(jnp.concatenate(pieces, axis=1), perm[...])
+        one, two = pieces
+        low = (iota(one.shape, 1) & 4) == 0
+        re = jnp.where(low, one, pltpu.roll(two, 4, 1)).astype(jnp.float32)
+        im = jnp.where(low, pltpu.roll(one, LANES - 4, 1), two).astype(jnp.float32)
         for j in range(size // RADIX):
             rows_at = pl.ds((start // RADIX + j) * PITCH, RADIX)
-            part = both[j * RADIX : (j + 1) * RADIX]
-            a_re[rows_at, :] = part[:, :LANES]
-            a_im[rows_at, :] = part[:, LANES:]
+            a_re[rows_at, :] = re[j * RADIX : (j + 1) * RADIX]
+            a_im[rows_at, :] = im[j * RADIX : (j + 1) * RADIX]
 
     for src in range(sources):
         unpack([rx[src, s] for s in slabs], NTAP + src * rows, rows)
@@ -172,33 +159,41 @@
     def loop(body):
         def many(step, carry):
             for j in range(unroll // PAIR):
-                body(step * unroll + j * PAIR)
+                body(step, j * PAIR)
             return carry
 
         lax.fori_loop(0, RADIX // unroll, many, 0)
 
-    def first_stage(i):
+    def twiddle(step, k):
+        shape = (RADIX, LANES)
+        return [jnp.broadcast_to(w[step, :, k : k + 1], shape) for w in (tw_c, tw_s)]
+
+    def first_stage(step, k):
+        i = step * unroll + k
         out = dot(fwd[...], columns(a_re, a_im, i))
         for j in range(PAIR):
             re, im = split(out, j)
-            cos, sin = tw_c[at_of(i + j), :], tw_s[at_of(i + j), :]
+            cos, sin = twiddle(step, k + j)
             b_re[pitched(i + j), :] = re * cos + im * sin
             b_im[pitched(i + j), :] = im * cos - re * sin
 
     loop(first_stage)
-
-    def middle_stages(i):
+    for copy in chirps:
+        copy.wait()
+
+    def middle_stages(step, k):
+        i = step * unroll + k
         out = dot(fwd[...], columns(b_re, b_im, i))
         filtered = []
         for j in range(PAIR):
             re, im = split(out, j)
-            cos, sin = ch_c[at_of(i + j), :], ch_s[at_of(i + j), :]
+            cos, sin = c_c[at_of(i + j), :], c_s[at_of(i + j), :]
             both = jnp.concatenate([re * cos + im * sin, im * cos - re * sin], axis=0)
             filtered.append(both.astype(jnp.bfloat16))
         out = dot(inv[...], jnp.concatenate(filtered, axis=1))
         for j in range(PAIR):
             re, im = split(out, j)
-            cos, sin = tw_c[at_of(i + j), :], tw_s[at_of(i + j), :]
+            cos, sin = twiddle(step, k + j)
             a_re[pitched(i + j), :] = re * cos - im * sin
             a_im[pitched(i + j), :] = im * cos + re * sin
 
@@ -206,29 +201,31 @@
 
     kept = last.shape[0] // 2
 
-    def last_stage(i):
+    def last_stage(step, k):
+        i = step * unroll + k
         out = dot(last[...], columns(a_re, a_im, i)) * (1.0 / NFFT)
         for j in range(PAIR):
             re, im = split(out, j)
             power = re * re + im * im
-            power = power + pltpu.roll(power, 64, 1)
+            power = power + pltpu.roll(power, LANES - 8 if slabs[0] == 0 else 8, 1)
             at = pl.ds(pl.multiple_of((i + j) * kept, 16), kept)
             o_ref[at, :] = power.astype(jnp.bfloat16)
 
     loop(last_stage)
 
 
-def detect(slabs, received, halo, tables, unroll=32):
+def detect(slabs, received, halo, tables):
     sources, _, rows, _ = received.shape
     span = sources * rows
     whole = pl.BlockSpec(memory_space=VMEM)
     args = [received, halo, *tables]
     flops = 2 * 2 * RADIX * 4 * 2 * RADIX * RADIX * LANES
     scratch = [VMEM((RADIX * PITCH, LANES), jnp.float32)] * 4
+    scratch += [VMEM((NFFT, LANES), jnp.float32)] * 2 + [pltpu.SemaphoreType.DMA((2,))]
     return pl.pallas_call(
-        functools.partial(detect_kernel, slabs, unroll),
+        functools.partial(detect_kernel, slabs),
         out_shape=jax.ShapeDtypeStruct((span, LANES), jnp.bfloat16),
-        in_specs=[whole] * len(args),
+        in_specs=[whole] * (len(args) - 2) + [pl.BlockSpec(memory_space=pl.ANY)] * 2,
         out_specs=whole,
         scratch_shapes=scratch,
         cost_estimate=pl.CostEstimate(flops=flops, bytes_accessed=16 << 20, transcendentals=0),
@@ -243,7 +240,7 @@
     lane = iota((LANES, LANES), 1)
     for t in range(span // LANES):
         at = pl.ds(t * LANES, LANES)
-        both = jnp.where(lane < 64, early[at, :].astype(jnp.float32), late[at, :].astype(jnp.float32))
+        both = jnp.where((lane & 8) == 0, early[at, :].astype(jnp.float32), late[at, :].astype(jnp.float32))
         turned[:, at] = both.T
     total = jnp.zeros((KEYS * GROUP, PAGE), jnp.float32)
     for q in range(QUADS):
@@ -253,9 +250,10 @@
             shape = (KEYS, chunk)
             mine = jnp.broadcast_to(code >> 8, shape) == iota(shape, 0)
             picked = []
-            for c in range(q * GROUP, (q + 1) * GROUP):
-                own = jnp.broadcast_to(turned[c : c + 1, at], shape)
-                picked.append(jnp.where(mine, own, 0.0))
+            for c in range(q * 4, LANES, 4 * QUADS):
+                for i in range(c, c + 4):
+                    own = jnp.broadcast_to(turned[i : i + 1, at], shape)
+                    picked.append(jnp.where(mine, own, 0.0))
             picked = jnp.concatenate(picked, axis=0).astype(jnp.bfloat16)
             low = jnp.broadcast_to(code & (PAGE - 1), (PAGE, chunk))
             onehot = jnp.where(low == iota((PAGE, chunk), 0), 1.0, 0.0).astype(jnp.bfloat16)
@@ -307,11 +305,11 @@
     keys = shared(mine)
     own = lax.axis_index("zl") * 2 + lax.axis_index("xh")
     rates = lax.dynamic_index_in_dim(chirp_rates.reshape(-1, QUADS, 4), own, 1, False)
-    rates = jnp.tile(rates.reshape(GROUP), LANES // GROUP)
-    tables = all_tables(rates)
+    rates = jnp.broadcast_to(rates[:, None, :], (GROUP // 4, 4, 4)).reshape(LANES)
+    tables = (*transform_tables(), *chirp_table(rates))
     first = (span - NTAP) // rows
     tail = received[first:, QUADS - 1].reshape(-1, LANES)[-NTAP:]
-    ready = jnp.maximum(tables[4][0, 0], tables[6][0, 0]) < 2.0
+    ready = tables[-1][0, 0] < 2.0
     tail = jnp.where(ready, tail, jnp.zeros_like(tail))
     blocks = lax.axis_size("zh")
     halo = lax.ppermute(tail, "zh", [(i, i + 1) for i in range(blocks - 1)])

time: 111 us -> 111 us (level)
  local copies, waits for them, and re-layouts: 17.4 us -> 5.7 us
  waiting for transfers between devices: 4.87 us -> 15.3 us
  blocking collectives: 32.7 us -> 35.5 us
    unnamed x26 -> x14, local copies, waits for them, and re-layouts: 15 us -> 3.19 us
    ppermute x1, waiting for transfers between devices: 2.62 us -> 13 us  [shared(): by_x = lax.ppermute(mine, 'xh', across)]
    cos x0 -> x1, other arithmetic: none -> 9.59 us  [chirp_table(): jnp.cos(phase).reshape(-1, LANES)]
    sin x2 -> x1, other arithmetic: 9.68 us -> 0.27 us  [transform_tables(): jnp.sin(twist)]
    all_to_all x1, blocking collectives: 32.7 us -> 35.5 us  [shards(): pieces = lax.all_to_all(pieces, 'zh', 0, 0, tiled=True)]
    pallas_call x3 -> x2, Pallas kernels: 10.3 us -> 10 us  [detect(): pl.pallas_call(functools.partial(detect_kernel, slabs), out_shape=jax.Sha...]
where the time goes in v4:
time: 111 us
  blocking collectives  35.5 us (32%)
  starting transfers between devices  25.3 us (23%)
  Pallas kernels  17.5 us (16%)
  waiting for transfers between devices  15.3 us (14%)
  other arithmetic  10.5 us (9%)
  local copies, waits for them, and re-layouts  5.7 us (5%)
    all_to_all x1, blocking collectives, shards(): pieces = lax.all_to_all(pieces, 'zh', 0, 0, tiled=True)  35.5 us
    ppermute x1, waiting for transfers between devices, shared(): by_x = lax.ppermute(mine, 'xh', across)  13 us
    all_to_all x1, starting transfers between devices, shards(): received = lax.all_to_all(packed, ('chan', 'zl', 'xh'), 0, 0, tiled=True)  10.2 us
    pallas_call x2, Pallas kernels, detect(): pl.pallas_call(functools.partial(detect_kernel, slabs), out_shape=jax.Sha...  10 us
    cos x1, other arithmetic, chirp_table(): jnp.cos(phase).reshape(-1, LANES)  9.59 us
    pallas_call x1, Pallas kernels, pack(): pl.pallas_call(functools.partial(pack_kernel, groups), out_shape=jax.Shap...  5.48 us
    ppermute x1, starting transfers between devices, shared(): by_both = lax.ppermute(mine, ('zl', 'xh'), both)  4.87 us
    ppermute x1, starting transfers between devices, shards(): halo = lax.ppermute(tail, 'zh', [(i, i + 1) for i in range(blocks - 1)])  4.41 us
  transfers between devices with their start and end apart: 5, of which 2 were waited for; matrix products, arithmetic and copies ran while one was open for 11% of the time, Pallas kernels for 5%

profile of v4, /device:TPU:8, one launch (start us, length us, event | category | flops | bytes accessed | tf_op | source)
XLA Modules:
  0.0 110.7 jit_solution(1195028906381378028)
XLA Ops:
  0.0 5.5 %pack.1 = bf16[64,192,128]{2,1,0:T(8,128)(2,1)} custom-call(bf16[2,2,1,192,2048]{4,3,2,1,0:T(8,128)(2,1)} %x_ref.1), custom_call_target="tpu_custom_call" | custom-call | tf_op jit(solution)/shard_map/pack/pallas_call | solution.py:90
  5.5 10.2 %all-to-all-start = ((bf16[64,192,128]{2,1,0:T(8,128)(2,1)}), bf16[64,192,128]{2,1,0:T(8,128)(2,1)S(1)}, u32[]{:S(2)}, u32[]{:S(2)}) async-start(bf16[64,192,128]{2,1,0:T(8,128)(2,1)} %pack.1), calls=%async_computation | async-start | bytes 6291456 | tf_op jit(solution)/shard_map/all_to_all | solution.py:300
  15.7 0.1 reshape.88
  15.8 0.1 copy.9
  15.9 0.1 reshape.89
  16.0 3.4 %collective-permute-start.2 = (s32[1,3072]{1,0:T(1,128)S(1)}, s32[1,3072]{1,0:T(1,128)S(1)}, u32[]{:S(2)}, u32[]{:S(2)}) collective-permute-start(s32[1,3072]{1,0:T(1,128)S(1)} %reshape.89), channel_id=1, source_target_pairs={{0,2},{2,0},{1,3},{3,1},{4,6},{6,4},{5,7},{7,5},{8,10},{10,8},{9,1... | collective-permute-start | bytes 36872 | tf_op jit(solution)/shard_map/ppermute | solution.py:289
  19.4 4.9 %collective-permute-start.3 = (s32[1,3072]{1,0:T(1,128)S(1)}, s32[1,3072]{1,0:T(1,128)S(1)}, u32[]{:S(2)}, u32[]{:S(2)}) collective-permute-start(s32[1,3072]{1,0:T(1,128)S(1)} %reshape.89), channel_id=1, source_target_pairs={{0,3},{1,2},{2,1},{3,0},{4,7},{5,6},{6,5},{7,4},{8,11},{9,10},{10,... | collective-permute-start | bytes 36872 | tf_op jit(solution)/shard_map/ppermute | solution.py:290
  24.3 2.5 %collective-permute-start.1 = (s32[1,3072]{1,0:T(1,128)S(1)}, s32[1,3072]{1,0:T(1,128)S(1)}, u32[]{:S(2)}, u32[]{:S(2)}) collective-permute-start(s32[1,3072]{1,0:T(1,128)S(1)} %reshape.89), channel_id=1, source_target_pairs={{0,1},{1,0},{2,3},{3,2},{4,5},{5,4},{6,7},{7,6},{8,9},{9,8},{10,11... | collective-permute-start | bytes 36872 | tf_op jit(solution)/shard_map/ppermute | solution.py:288
  26.8 0.1 add.115
  26.9 0.1 add.117
  26.9 0.1 reshape.87
  27.1 0.1 mul.183
  27.2 0.1 fusion.27
  27.4 0.2 sine_convert_fusion
  27.5 0.1 fusion.12
  27.6 0.3 fusion.16
  27.9 9.6 %fusion.1 = (f32[4096,128]{1,0:T(8,128)}, f32[4096,128]{1,0:T(8,128)}) fusion(f32[4096]{0:T(1024)S(1)} %fusion.26, f32[128]{0:T(128)S(1)} %mul.183), kind=kLoop, calls=%fused_computation.2 | loop fusion | flops 2097152 | bytes 4211200 | tf_op jit(solution)/shard_map/cos | solution.py:56
  37.5 0.1 fusion.22.last
  37.6 1.2 %slice.20 = f32[1,1]{1,0:T(1,128)} slice(f32[4096,128]{1,0:T(8,128)} %get-tuple-element.14.ch_s), slice={[0:1], [0:1]} | slice | bytes 8 | tf_op jit(solution)/shard_map/slice | solution.py:312
  39.4 13.0 %collective-permute-done.1 = s32[1,3072]{1,0:T(1,128)S(1)} collective-permute-done((s32[1,3072]{1,0:T(1,128)S(1)}, s32[1,3072]{1,0:T(1,128)S(1)}, u32[]{:S(2)}, u32[]{:S(2)}) %collective-permute-start.1) | collective-permute-done | bytes 12320 | tf_op jit(solution)/shard_map/ppermute | solution.py:288
  52.5 0.0 collective-permute-done.2
  52.5 2.2 %collective-permute-done.3 = s32[1,3072]{1,0:T(1,128)S(1)} collective-permute-done((s32[1,3072]{1,0:T(1,128)S(1)}, s32[1,3072]{1,0:T(1,128)S(1)}, u32[]{:S(2)}, u32[]{:S(2)}) %collective-permute-start.3) | collective-permute-done | bytes 12320 | tf_op jit(solution)/shard_map/ppermute | solution.py:290
  54.8 0.0 all-to-all-done
  54.9 4.4 %collective-permute-start = (bf16[1024,128]{1,0:T(8,128)(2,1)S(1)}, bf16[1024,128]{1,0:T(8,128)(2,1)S(1)}, u32[]{:S(2)}, u32[]{:S(2)}) collective-permute-start(bf16[1024,128]{1,0:T(8,128)(2,1)S(1)} %slice_select_fusion.halo), channel_id=1, source_target_pairs={{0,4},{4,8},{8,12},{12,16},{16,20},{20,24},{24,28},{1,5},{5,9},{9,... | collective-permute-start | bytes 786440 | tf_op jit(solution)/shard_map/ppermute | solution.py:315
  59.4 1.6 %copy-done = f32[4096,128]{1,0:T(8,128)S(1)} copy-done((f32[4096,128]{1,0:T(8,128)S(1)}, f32[4096,128]{1,0:T(8,128)}, u32[]{:S(2)}) %copy-start) | copy-done | bytes 2097176
  60.9 1.6 %copy-done.2 = f32[4096,128]{1,0:T(8,128)S(1)} copy-done((f32[4096,128]{1,0:T(8,128)S(1)}, f32[4096,128]{1,0:T(8,128)}, u32[]{:S(2)}) %copy-start.2) | copy-done | bytes 2097176
  62.5 5.0 %detect.2.late = bf16[3072,128]{1,0:T(8,128)(2,1)S(1)} custom-call(bf16[16,4,192,128]{3,2,1,0:T(8,128)(2,1)S(1)} %bitcast.7, bf16[1024,128]{1,0:T(8,128)(2,1)S(1)} %slice_select_fusion.halo, bf16[128,128]{1,0:T(8,128)(2,1)S(1)} %get-tuple-element.8.fwd, bf16[128,128]{1,0:T(8,128)(2,1)S(1)} %get-tuple-element.7.inv, bf16[96,128]{1,0:T(8,128)(2,1)S(1)} %fusion.22.last, ...), custom_call_target="tpu_custom_call" | custom-call | flops 1073741824 | bytes 16777216 | tf_op jit(solution)/shard_map/detect/pallas_call | solution.py:225
  67.5 0.0 collective-permute-done.halo
  67.6 5.0 %detect.3.early = bf16[3072,128]{1,0:T(8,128)(2,1)S(1)} custom-call(bf16[16,4,192,128]{3,2,1,0:T(8,128)(2,1)S(1)} %bitcast.8, bf16[1024,128]{1,0:T(8,128)(2,1)S(1)} %collective-permute-done.halo, bf16[128,128]{1,0:T(8,128)(2,1)S(1)} %get-tuple-element.8.fwd, bf16[128,128]{1,0:T(8,128)(2,1)S(1)} %get-tuple-element.7.inv, bf16[96,128]{1,0:T(8,128)(2,1)S(1)} %fusion.22.last, ...), custom_call_target="tpu_custom_call" | custom-call | flops 1073741824 | bytes 16777216 | tf_op jit(solution)/shard_map/detect/pallas_call | solution.py:225
  72.6 2.0 %fold.1 = bf16[256,256]{1,0:T(8,128)(2,1)S(1)} custom-call(bf16[3072,128]{1,0:T(8,128)(2,1)S(1)} %detect.2.late, bf16[3072,128]{1,0:T(8,128)(2,1)S(1)} %detect.3.early, s32[4,3072]{1,0:T(4,128)S(1)} %pad_add_fusion.keys), custom_call_target="tpu_custom_call" | custom-call | flops 1610612736 | bytes 8388608 | tf_op jit(solution)/shard_map/fold/pallas_call | solution.py:273
  74.6 35.5 %all_to_all.10 = bf16[8,32,256]{2,1,0:T(8,128)(2,1)S(1)} all-to-all(bf16[8,32,256]{2,1,0:T(8,128)(2,1)S(1)} %bitcast.9), channel_id=1, replica_groups=mesh['chan'=16,'zh'=8,'zl'=2,'xh'=2] {'zh'}, dimensions={0} | all-to-all | bytes 262144 | tf_op jit(solution)/shard_map/all_to_all | solution.py:320
  110.1 0.6 mul.207
  (28 shorter events, 0.3 us)
Async XLA Ops:
  5.5 10.2 %copy-start.4 = (s32[3072]{0:T(1024)S(1)}, s32[3072]{0:T(1024)}, u32[]{:S(2)}) copy-start(s32[3072]{0:T(1024)} %param.6) | copy-start | bytes 36868
  5.5 10.2 %copy-start.5 = (s32[3072]{0:T(1024)S(1)}, s32[3072]{0:T(1024)}, u32[]{:S(2)}) copy-start(s32[3072]{0:T(1024)} %param.7) | copy-start | bytes 36868
  5.5 21.5 %copy-start.6 = (f32[128]{0:T(128)S(1)}, f32[128]{0:T(128)}, u32[]{:S(2)}) copy-start(f32[128]{0:T(128)} %param.5) | copy-start | bytes 1540
  5.5 49.3 %all-to-all-start = ((bf16[64,192,128]{2,1,0:T(8,128)(2,1)}), bf16[64,192,128]{2,1,0:T(8,128)(2,1)S(1)}, u32[]{:S(2)}, u32[]{:S(2)}) async-start(bf16[64,192,128]{2,1,0:T(8,128)(2,1)} %pack.1), calls=%async_computation | async-start | bytes 6291456 | tf_op jit(solution)/shard_map/all_to_all | solution.py:300
  16.0 36.5 %collective-permute-start.2 = (s32[1,3072]{1,0:T(1,128)S(1)}, s32[1,3072]{1,0:T(1,128)S(1)}, u32[]{:S(2)}, u32[]{:S(2)}) collective-permute-start(s32[1,3072]{1,0:T(1,128)S(1)} %reshape.89), channel_id=1, source_target_pairs={{0,2},{2,0},{1,3},{3,1},{4,6},{6,4},{5,7},{7,5},{8,10},{10,8},{9,1... | collective-permute-start | bytes 36872 | tf_op jit(solution)/shard_map/ppermute | solution.py:289
  19.4 35.4 %collective-permute-start.3 = (s32[1,3072]{1,0:T(1,128)S(1)}, s32[1,3072]{1,0:T(1,128)S(1)}, u32[]{:S(2)}, u32[]{:S(2)}) collective-permute-start(s32[1,3072]{1,0:T(1,128)S(1)} %reshape.89), channel_id=1, source_target_pairs={{0,3},{1,2},{2,1},{3,0},{4,7},{5,6},{6,5},{7,4},{8,11},{9,10},{10,... | collective-permute-start | bytes 36872 | tf_op jit(solution)/shard_map/ppermute | solution.py:290
  24.3 28.2 %collective-permute-start.1 = (s32[1,3072]{1,0:T(1,128)S(1)}, s32[1,3072]{1,0:T(1,128)S(1)}, u32[]{:S(2)}, u32[]{:S(2)}) collective-permute-start(s32[1,3072]{1,0:T(1,128)S(1)} %reshape.89), channel_id=1, source_target_pairs={{0,1},{1,0},{2,3},{3,2},{4,5},{5,4},{6,7},{7,6},{8,9},{9,8},{10,11... | collective-permute-start | bytes 36872 | tf_op jit(solution)/shard_map/ppermute | solution.py:288
  54.9 12.7 %collective-permute-start = (bf16[1024,128]{1,0:T(8,128)(2,1)S(1)}, bf16[1024,128]{1,0:T(8,128)(2,1)S(1)}, u32[]{:S(2)}, u32[]{:S(2)}) collective-permute-start(bf16[1024,128]{1,0:T(8,128)(2,1)S(1)} %slice_select_fusion.halo), channel_id=1, source_target_pairs={{0,4},{4,8},{8,12},{12,16},{16,20},{20,24},{24,28},{1,5},{5,9},{9,... | collective-permute-start | bytes 786440 | tf_op jit(solution)/shard_map/ppermute | solution.py:315
  59.3 1.6 %copy-start = (f32[4096,128]{1,0:T(8,128)S(1)}, f32[4096,128]{1,0:T(8,128)}, u32[]{:S(2)}) copy-start(f32[4096,128]{1,0:T(8,128)} %get-tuple-element.13.ch_c) | copy-start | bytes 6291460
  60.9 1.6 %copy-start.2 = (f32[4096,128]{1,0:T(8,128)S(1)}, f32[4096,128]{1,0:T(8,128)}, u32[]{:S(2)}) copy-start(f32[4096,128]{1,0:T(8,128)} %get-tuple-element.14.ch_s) | copy-start | bytes 6291460
  62.5 5.0 %copy-start.1 = (f32[4096,128]{1,0:T(8,128)S(1)}, f32[4096,128]{1,0:T(8,128)}, u32[]{:S(2)}) copy-start(f32[4096,128]{1,0:T(8,128)} %get-tuple-element.13.ch_c) | copy-start | bytes 6291460
  62.5 5.0 %copy-start.3 = (f32[4096,128]{1,0:T(8,128)S(1)}, f32[4096,128]{1,0:T(8,128)}, u32[]{:S(2)}) copy-start(f32[4096,128]{1,0:T(8,128)} %get-tuple-element.14.ch_s) | copy-start | bytes 6291460

commit v5 on v4

v5 whole, which is shorter than its diff:
```python
import functools
import math

import jax
import jax.numpy as jnp
import numpy as np
from jax import lax
from jax.experimental import pallas as pl
from jax.experimental.pallas import tpu as pltpu
from jax.sharding import Mesh
from jax.sharding import PartitionSpec as P

RADIX = 64
BINS = 1024
NSUB = 2
NFFT = 4096
NTAP = 1024
LANES = 128
GROUP = 32
QUADS = 4
PAGE = 256
KEYS = NSUB * BINS // PAGE
VMEM = pltpu.VMEM
GRANT = 20 << 20
UNROLL = 32


def real_form(cosine, sine):
    top = jnp.concatenate([cosine, sine], axis=1)
    bottom = jnp.concatenate([-sine, cosine], axis=1)
    return jnp.concatenate([top, bottom], axis=0)


def transform_tables():
    indices = jnp.arange(RADIX, dtype=jnp.int32)
    small = indices[:, None] * indices[None, :] % RADIX
    angles = 2.0 * math.pi / RADIX * small.astype(jnp.float32)
    cosine = jnp.cos(angles).astype(jnp.bfloat16)
    sine = jnp.sin(angles).astype(jnp.bfloat16)
    forward = real_form(cosine, sine)
    inverse = real_form(cosine, -sine)
    first = NTAP // RADIX
    last = jnp.concatenate([inverse[first:RADIX], inverse[RADIX + first :]], axis=0)
    large = indices[:, None] * indices[None, :] % NFFT
    twist = 2.0 * math.pi / NFFT * large.astype(jnp.float32)
    return (forward, inverse, last), (jnp.cos(twist), jnp.sin(twist))


def chirp_table(rates_here):
    indices = jnp.arange(RADIX, dtype=jnp.int32)
    spectral = indices[:, None] + RADIX * indices[None, :]
    offset = ((spectral + NFFT // 2) % NFFT).astype(jnp.float32) / NFFT
    turns = rates_here[None, None, :] * (offset * offset)[:, :, None]
    phase = 2.0 * math.pi * (turns - jnp.floor(turns))
    return jnp.cos(phase).reshape(-1, LANES), jnp.sin(phase).reshape(-1, LANES)


def spread_kernel(cos, sin, wide_cos, wide_sin):
    for i in range(RADIX):
        at = pl.ds(i * RADIX, RADIX)
        wide_cos[at, :] = jnp.broadcast_to(cos[:, i : i + 1], (RADIX, LANES))
        wide_sin[at, :] = jnp.broadcast_to(sin[:, i : i + 1], (RADIX, LANES))


def all_tables(rates):
    matrices, twiddles = transform_tables()
    whole = pl.BlockSpec(memory_space=VMEM)
    spread = pl.pallas_call(
        spread_kernel,
        out_shape=[jax.ShapeDtypeStruct((NFFT, LANES), jnp.float32)] * 2,
        in_specs=[whole] * 2,
        out_specs=[whole] * 2,
        compiler_params=pltpu.CompilerParams(vmem_limit_bytes=GRANT),
        name="spread",
    )(*twiddles)
    return (*matrices, *spread, *chirp_table(rates))


def iota(shape, axis):
    return lax.broadcasted_iota(jnp.int32, shape, axis)


def dot(a, b):
    return jnp.dot(a, b, preferred_element_type=jnp.float32)


def pack_kernel(groups, x_ref, perm_ref, o_ref):
    lane = iota((x_ref.shape[3], LANES), 1)
    for g in range(groups):
        lanes = pl.ds(g * LANES, LANES)
        parts = [x_ref[p, r, 0, :, lanes] for p in range(2) for r in range(2)]
        if g % 2 == 0:
            out = dot(jnp.concatenate(parts, axis=1), perm_ref[...]).astype(jnp.bfloat16)
            parts = [out[:, q * LANES : (q + 1) * LANES] for q in range(QUADS)]
        else:
            for bit in range(2):
                step = 4 << bit
                low = (lane & step) == 0
                for s in range(4):
                    if s & (1 << bit) == 0:
                        t = s | (1 << bit)
                        parts[s], parts[t] = (
                            jnp.where(low, parts[s], pltpu.roll(parts[t], step, 1)),
                            jnp.where(low, pltpu.roll(parts[s], LANES - step, 1), parts[t]),
                        )
        for q in range(QUADS):
            o_ref[g * QUADS + q] = parts[q]


def moved(target):
    row = np.arange(target.size)
    return jnp.asarray(target[:, None] == row[None, :], dtype=jnp.bfloat16)


def pack_moves():
    row = np.arange(QUADS * LANES)
    part, rest = row >> 7, row & 127
    return moved((rest >> 2 & 3) * LANES + (rest & 0x73) + part * 4)


def pack(capture, groups=8):
    rows, channels = capture.shape[3:]
    chans = channels // LANES
    wide = QUADS * LANES
    return pl.pallas_call(
        functools.partial(pack_kernel, groups),
        out_shape=jax.ShapeDtypeStruct((chans * QUADS, rows, LANES), jnp.bfloat16),
        grid=(chans // groups,),
        in_specs=[
            pl.BlockSpec((2, 2, 1, rows, groups * LANES), lambda g: (0, 0, 0, 0, g)),
            pl.BlockSpec((wide, wide), lambda g: (0, 0)),
        ],
        out_specs=pl.BlockSpec((groups * QUADS, rows, LANES), lambda g: (g, 0, 0)),
        name="pack",
    )(capture, pack_moves())


PAIR = 2
PITCH = 68


def detect_kernel(slabs, *refs):
    carried = None if slabs[0] > 0 else refs[0]
    rx, halo, keys, fwd, inv, last, tw_c, tw_s, ch_c, ch_s, o_ref = refs[-17:-6]
    a_re, a_im, b_re, b_im, powers, turned = refs[-6:]
    unroll = UNROLL
    sources, _, rows, _ = rx.shape
    span = sources * rows
    tail = span - NTAP

    def unpack(pieces, start, size):
        low = (iota((RADIX, LANES), 1) & 4) == 0
        for j in range(size // RADIX):
            rows_at = pl.ds((start // RADIX + j) * PITCH, RADIX)
            one, two = [piece(j * RADIX).astype(jnp.float32) for piece in pieces]
            a_re[rows_at, :] = jnp.where(low, one, pltpu.roll(two, 4, 1))
            a_im[rows_at, :] = jnp.where(low, pltpu.roll(one, LANES - 4, 1), two)

    def from_slab(src, s, first, j):
        return rx[src, s, pl.ds(first + j, RADIX), :]

    def from_halo(first, j):
        return halo[pl.ds(first + j, RADIX), :]

    partial = functools.partial
    for src in range(sources):
        unpack([partial(from_slab, src, s, 0) for s in slabs], NTAP + src * rows, rows)
        low = max(tail, src * rows)
        size = (src + 1) * rows - low
        if size > 0:
            skip = low - src * rows
            before = [
                partial(from_halo, low - tail) if s == 0 else partial(from_slab, src, s - 1, skip)
                for s in slabs
            ]
            unpack(before, low - tail, size)

    def column(re, im, i):
        at = pl.ds(i, RADIX, stride=PITCH)
        return jnp.concatenate([re[at, :], im[at, :]], axis=0).astype(jnp.bfloat16)

    def columns(re, im, i):
        return jnp.concatenate([column(re, im, i + j) for j in range(PAIR)], axis=1)

    def split(out, j):
        half = out.shape[0] // 2
        own = out[:, j * LANES : (j + 1) * LANES]
        return own[:half], own[half:]

    def at_of(i):
        return pl.ds(pl.multiple_of(i * RADIX, RADIX), RADIX)

    def pitched(i):
        return pl.ds(i * PITCH, RADIX)

    def loop(body):
        def many(step, carry):
            for j in range(unroll // PAIR):
                body(step, j * PAIR)
            return carry

        lax.fori_loop(0, RADIX // unroll, many, 0)

    def twiddle(i):
        return tw_c[at_of(i), :], tw_s[at_of(i), :]

    def first_stage(step, k):
        i = step * unroll + k
        out = dot(fwd[...], columns(a_re, a_im, i))
        for j in range(PAIR):
            re, im = split(out, j)
            cos, sin = twiddle(i + j)
            b_re[pitched(i + j), :] = re * cos + im * sin
            b_im[pitched(i + j), :] = im * cos - re * sin

    loop(first_stage)

    def middle_stages(step, k):
        i = step * unroll + k
        out = dot(fwd[...], columns(b_re, b_im, i))
        filtered = []
        for j in range(PAIR):
            re, im = split(out, j)
            cos, sin = ch_c[at_of(i + j), :], ch_s[at_of(i + j), :]
            both = jnp.concatenate([re * cos + im * sin, im * cos - re * sin], axis=0)
            filtered.append(both.astype(jnp.bfloat16))
        out = dot(inv[...], jnp.concatenate(filtered, axis=1))
        for j in range(PAIR):
            re, im = split(out, j)
            cos, sin = twiddle(i + j)
            a_re[pitched(i + j), :] = re * cos - im * sin
            a_im[pitched(i + j), :] = im * cos + re * sin

    loop(middle_stages)

    kept = last.shape[0] // 2

    def last_stage(step, k):
        i = step * unroll + k
        out = dot(last[...], columns(a_re, a_im, i)) * (1.0 / NFFT)
        for j in range(PAIR):
            re, im = split(out, j)
            power = re * re + im * im
            power = power + pltpu.roll(power, LANES - 8 if slabs[0] == 0 else 8, 1)
            at = pl.ds(pl.multiple_of((i + j) * kept, 16), kept)
            powers[at, :] = power.astype(jnp.bfloat16)

    loop(last_stage)

    for t in range(span // LANES):
        at = pl.ds(t * LANES, LANES)
        turned[:, at] = powers[at, :].astype(jnp.float32).T
    chunk = 512
    total = jnp.zeros((KEYS * GROUP, PAGE), jnp.float32) if carried is None else carried[...]
    for q in slabs:
        for t in range(span // chunk):
            at = pl.ds(t * chunk, chunk)
            code = keys[q : q + 1, at]
            shape = (KEYS, chunk)
            mine = jnp.broadcast_to(code >> 8, shape) == iota(shape, 0)
            picked = []
            for c in range(q * 4, LANES, 4 * QUADS):
                for i in range(c, c + 4):
                    own = jnp.broadcast_to(turned[i : i + 1, at], shape)
                    picked.append(jnp.where(mine, own, 0.0))
            picked = jnp.concatenate(picked, axis=0).astype(jnp.bfloat16)
            low = jnp.broadcast_to(code & (PAGE - 1), (PAGE, chunk))
            onehot = jnp.where(low == iota((PAGE, chunk), 0), 1.0, 0.0).astype(jnp.bfloat16)
            total = total + lax.dot_general(
                picked,
                onehot,
                (((1,), (1,)), ((), ())),
                preferred_element_type=jnp.float32,
            )
    o_ref[...] = total.astype(o_ref.dtype)


def detect(slabs, received, halo, keys, tables, carried=None):
    sources, _, rows, _ = received.shape
    span = sources * rows
    whole = pl.BlockSpec(memory_space=VMEM)
    args = [received, halo, keys, *tables]
    if carried is not None:
        args = [carried, *args]
    kind = jnp.float32 if carried is None else jnp.bfloat16
    flops = 2 * 2 * RADIX * 4 * 2 * RADIX * RADIX * LANES
    scratch = [VMEM((RADIX * PITCH, LANES), jnp.float32)] * 4
    scratch += [VMEM((span, LANES), jnp.bfloat16), VMEM((LANES, span), jnp.float32)]
    return pl.pallas_call(
        functools.partial(detect_kernel, slabs),
        out_shape=jax.ShapeDtypeStruct((KEYS * GROUP, PAGE), kind),
        in_specs=[whole] * len(args),
        out_specs=whole,
        scratch_shapes=scratch,
        cost_estimate=pl.CostEstimate(flops=flops, bytes_accessed=16 << 20, transcendentals=0),
        compiler_params=pltpu.CompilerParams(vmem_limit_bytes=GRANT),
        name="detect",
    )(*args)


def shared(mine):
    across = [(0, 1), (1, 0)]
    both = [(0, 3), (1, 2), (2, 1), (3, 0)]
    by_x = lax.ppermute(mine, "xh", across)
    by_z = lax.ppermute(mine, "zl", across)
    by_both = lax.ppermute(mine, ("zl", "xh"), both)
    x_low, z_low = lax.axis_index("xh") == 0, lax.axis_index("zl") == 0
    near = jnp.concatenate([jnp.where(x_low, mine, by_x), jnp.where(x_low, by_x, mine)])
    far = jnp.concatenate([jnp.where(x_low, by_z, by_both), jnp.where(x_low, by_both, by_z)])
    return jnp.concatenate([jnp.where(z_low, near, far), jnp.where(z_low, far, near)])


def shards(capture, chirp_rates, phase_bin, sub_id):
    rows = capture.shape[3]
    packed = pack(capture)
    received = lax.all_to_all(packed, ("chan", "zl", "xh"), 0, 0, tiled=True)
    received = received.reshape(-1, QUADS, rows, LANES)

    span = phase_bin.shape[0]
    mine = (sub_id * BINS + phase_bin).reshape(span // RADIX, RADIX).T.reshape(1, span)
    keys = shared(mine)
    own = lax.axis_index("zl") * 2 + lax.axis_index("xh")
    rates = lax.dynamic_index_in_dim(chirp_rates.reshape(-1, QUADS, 4), own, 1, False)
    rates = jnp.broadcast_to(rates[:, None, :], (GROUP // 4, 4, 4)).reshape(LANES)
    tables = all_tables(rates)
    first = (span - NTAP) // rows
    tail = received[first:, QUADS - 1].reshape(-1, LANES)[-NTAP:]
    ready = jnp.maximum(tables[3][0, 0], tables[5][0, 0]) < 2.0
    tail = jnp.where(ready, tail, jnp.zeros_like(tail))
    blocks = lax.axis_size("zh")
    halo = lax.ppermute(tail, "zh", [(i, i + 1) for i in range(blocks - 1)])
    late = detect((2, 3), received, tail, keys, tables)
    partial = detect((0, 1), received, halo, keys, tables, late)
    pieces = partial.reshape(blocks, 4 * KEYS, PAGE)
    pieces = lax.all_to_all(pieces, "zh", 0, 0, tiled=True)
    scale = NSUB * BINS / (4.0 * span * blocks * QUADS)
    summed = jnp.sum(pieces.astype(jnp.float32), axis=0) * scale
    return summed.reshape(4, NSUB, BINS)


def solution(mesh):
    chans, slabs = mesh.devices.shape
    fine = Mesh(mesh.devices.reshape(chans, slabs // QUADS, 2, 2), ("chan", "zh", "zl", "xh"))
    slab = ("zh", "zl", "xh")
    placed = (P(None, None, slab, "chan", None), P("chan"), P(slab), P(slab))
    return jax.shard_map(
        shards,
        mesh=fine,
        in_specs=placed,
        out_specs=P(("chan", *slab), None, None),
        check_vma=False,
    )
```

time: 111 us -> 108 us (0.973)
  local copies, waits for them, and re-layouts: 5.7 us -> 12.1 us
  waiting for transfers between devices: 15.3 us -> 10.4 us
  blocking collectives: 35.5 us -> 31.6 us
  Pallas kernels: 17.5 us -> 16.3 us
    cos x1 -> x0, other arithmetic: 9.59 us -> none  [chirp_table(): jnp.cos(phase).reshape(-1, LANES)]
    sin x1 -> x2, other arithmetic: 0.27 us -> 9.67 us  [the longest x1 9.52 us: chirp_table(): jnp.sin(phase).reshape(-1, LANES)]
    unnamed x14 -> x22, local copies, waits for them, and re-layouts: 3.19 us -> 9.08 us
    ppermute x1, waiting for transfers between devices: 13 us -> 8.14 us  [shared(): by_x = lax.ppermute(mine, 'xh', across)]
    all_to_all x1, blocking collectives: 35.5 us -> 31.6 us  [shards(): pieces = lax.all_to_all(pieces, 'zh', 0, 0, tiled=True)]
    pallas_call x1, Pallas kernels: 5.48 us -> 4.08 us  [pack(): pl.pallas_call(functools.partial(pack_kernel, groups), out_shape=jax.Shap...]
  transfers between devices with their start and end apart: 5 -> 5, of which waited for: 2 -> 2; matrix products, arithmetic and copies ran while one was open for 11% -> 12% of each run, Pallas kernels for 5% -> 6%
where the time goes in v5:
time: 108 us
  blocking collectives  31.6 us (29%)
  starting transfers between devices  25.5 us (24%)
  Pallas kernels  16.3 us (15%)
  local copies, waits for them, and re-layouts  12.1 us (11%)
  waiting for transfers between devices  10.4 us (10%)
  other arithmetic  10.3 us (10%)
  between operations  1.56 us (1%)
    all_to_all x1, blocking collectives, shards(): pieces = lax.all_to_all(pieces, 'zh', 0, 0, tiled=True)  31.6 us
    pallas_call x2, Pallas kernels, detect(): pl.pallas_call(functools.partial(detect_kernel, slabs), out_shape=jax.Sha...  10.9 us
    all_to_all x1, starting transfers between devices, shards(): received = lax.all_to_all(packed, ('chan', 'zl', 'xh'), 0, 0, tiled=True)  10.2 us
    sin x1, other arithmetic, chirp_table(): jnp.sin(phase).reshape(-1, LANES)  9.52 us
    unnamed x22, local copies, waits for them, and re-layouts  9.08 us
    ppermute x1, waiting for transfers between devices, shared(): by_x = lax.ppermute(mine, 'xh', across)  8.14 us
    ppermute x1, starting transfers between devices, shared(): by_both = lax.ppermute(mine, ('zl', 'xh'), both)  4.87 us
    ppermute x1, starting transfers between devices, shards(): halo = lax.ppermute(tail, 'zh', [(i, i + 1) for i in range(blocks - 1)])  4.58 us
  transfers between devices with their start and end apart: 5, of which 2 were waited for; matrix products, arithmetic and copies ran while one was open for 12% of the time, Pallas kernels for 6%

profile of v5, /device:TPU:8, one launch (start us, length us, event | category | flops | bytes accessed | tf_op | source)
XLA Modules:
  0.0 107.8 jit_solution(1401256139411764304)
XLA Ops:
  0.0 4.1 %pack.1 = bf16[64,192,128]{2,1,0:T(8,128)(2,1)} custom-call(bf16[2,2,1,192,2048]{4,3,2,1,0:T(8,128)(2,1)} %x_ref.1, bf16[512,512]{1,0:T(8,128)(2,1)} %constant.70.clone.perm_ref), custom_call_target="tpu_custom_call" | custom-call | tf_op jit(solution)/shard_map/pack/pallas_call | solution.py:125
  4.1 10.2 %all-to-all-start = ((bf16[64,192,128]{2,1,0:T(8,128)(2,1)}), bf16[64,192,128]{2,1,0:T(8,128)(2,1)S(1)}, u32[]{:S(2)}, u32[]{:S(2)}) async-start(bf16[64,192,128]{2,1,0:T(8,128)(2,1)} %pack.1), calls=%async_computation | async-start | bytes 6291456 | tf_op jit(solution)/shard_map/all_to_all | solution.py:316
  14.4 0.1 copy.10
  14.5 0.1 reshape.70
  14.6 3.4 %collective-permute-start.1 = (s32[1,3072]{1,0:T(1,128)S(1)}, s32[1,3072]{1,0:T(1,128)S(1)}, u32[]{:S(2)}, u32[]{:S(2)}) collective-permute-start(s32[1,3072]{1,0:T(1,128)S(1)} %reshape.70), channel_id=1, source_target_pairs={{0,2},{2,0},{1,3},{3,1},{4,6},{6,4},{5,7},{7,5},{8,10},{10,8},{9,1... | collective-permute-start | bytes 36872 | tf_op jit(solution)/shard_map/ppermute | solution.py:305
  18.0 4.9 %collective-permute-start.2 = (s32[1,3072]{1,0:T(1,128)S(1)}, s32[1,3072]{1,0:T(1,128)S(1)}, u32[]{:S(2)}, u32[]{:S(2)}) collective-permute-start(s32[1,3072]{1,0:T(1,128)S(1)} %reshape.70), channel_id=1, source_target_pairs={{0,3},{1,2},{2,1},{3,0},{4,7},{5,6},{6,5},{7,4},{8,11},{9,10},{10,... | collective-permute-start | bytes 36872 | tf_op jit(solution)/shard_map/ppermute | solution.py:306
  22.9 2.5 %collective-permute-start = (s32[1,3072]{1,0:T(1,128)S(1)}, s32[1,3072]{1,0:T(1,128)S(1)}, u32[]{:S(2)}, u32[]{:S(2)}) collective-permute-start(s32[1,3072]{1,0:T(1,128)S(1)} %reshape.70), channel_id=1, source_target_pairs={{0,1},{1,0},{2,3},{3,2},{4,5},{5,4},{6,7},{7,6},{8,9},{9,8},{10,11... | collective-permute-start | bytes 36872 | tf_op jit(solution)/shard_map/ppermute | solution.py:304
  25.4 0.1 reshape.68
  25.5 0.1 mul.174
  25.7 0.1 mul.177
  25.8 0.1 fusion.26
  26.0 0.2 sine_convert_fusion
  26.1 0.1 fusion.24
  26.3 0.1 fusion.6
  26.4 9.5 %fusion.1 = (f32[4096,128]{1,0:T(8,128)}, f32[4096,128]{1,0:T(8,128)}) fusion(f32[4096]{0:T(1024)S(1)} %fusion.23, f32[128]{0:T(128)S(1)} %mul.174), kind=kLoop, calls=%fused_computation.2 | loop fusion | flops 2097152 | bytes 4211200 | tf_op jit(solution)/shard_map/sin | solution.py:55
  35.9 0.1 fusion.19.refs_5_.refs_6_
  36.0 1.2 %spread.1 = (f32[4096,128]{1,0:T(8,128)S(1)}, f32[4096,128]{1,0:T(8,128)S(1)}) custom-call(f32[64,64]{1,0:T(8,128)S(1)} %get-tuple-element.20.cos, f32[64,64]{1,0:T(8,128)S(1)} %get-tuple-element.19.sin), custom_call_target="tpu_custom_call" | custom-call | tf_op jit(solution)/shard_map/spread/pallas_call | solution.py:68
  37.2 1.4 %copy-done.6 = f32[4096,128]{1,0:T(8,128)} copy-done((f32[4096,128]{1,0:T(8,128)}, f32[4096,128]{1,0:T(8,128)S(1)}, u32[]{:S(2)}) %copy-start.6) | copy-done | bytes 2097176
  38.6 0.5 slice.18
  39.2 1.3 %copy-done.4 = f32[4096,128]{1,0:T(8,128)} copy-done((f32[4096,128]{1,0:T(8,128)}, f32[4096,128]{1,0:T(8,128)S(1)}, u32[]{:S(2)}) %copy-start.4) | copy-done | bytes 2097176
  40.5 1.2 %slice.24 = f32[1,1]{1,0:T(1,128)} slice(f32[4096,128]{1,0:T(8,128)} %get-tuple-element.18.refs_8_.refs_9_), slice={[0:1], [0:1]} | slice | bytes 8 | tf_op jit(solution)/shard_map/slice | solution.py:328
  42.9 8.1 %collective-permute-done = s32[1,3072]{1,0:T(1,128)S(1)} collective-permute-done((s32[1,3072]{1,0:T(1,128)S(1)}, s32[1,3072]{1,0:T(1,128)S(1)}, u32[]{:S(2)}, u32[]{:S(2)}) %collective-permute-start) | collective-permute-done | bytes 12320 | tf_op jit(solution)/shard_map/ppermute | solution.py:304
  51.1 2.2 %collective-permute-done.2 = s32[1,3072]{1,0:T(1,128)S(1)} collective-permute-done((s32[1,3072]{1,0:T(1,128)S(1)}, s32[1,3072]{1,0:T(1,128)S(1)}, u32[]{:S(2)}, u32[]{:S(2)}) %collective-permute-start.2) | collective-permute-done | bytes 12320 | tf_op jit(solution)/shard_map/ppermute | solution.py:306
  53.5 4.6 %collective-permute-start.3 = (bf16[1024,128]{1,0:T(8,128)(2,1)S(1)}, bf16[1024,128]{1,0:T(8,128)(2,1)S(1)}, u32[]{:S(2)}, u32[]{:S(2)}) collective-permute-start(bf16[1024,128]{1,0:T(8,128)(2,1)S(1)} %slice_select_fusion.refs_1_), channel_id=1, source_target_pairs={{0,4},{4,8},{8,12},{12,16},{16,20},{20,24},{24,28},{1,5},{5,9},{9,... | collective-permute-start | bytes 786440 | tf_op jit(solution)/shard_map/ppermute | solution.py:331
  58.1 1.6 %copy-done = f32[4096,128]{1,0:T(8,128)S(1)} copy-done((f32[4096,128]{1,0:T(8,128)S(1)}, f32[4096,128]{1,0:T(8,128)}, u32[]{:S(2)}) %copy-start) | copy-done | bytes 2097176
  59.7 1.6 %copy-done.2 = f32[4096,128]{1,0:T(8,128)S(1)} copy-done((f32[4096,128]{1,0:T(8,128)S(1)}, f32[4096,128]{1,0:T(8,128)}, u32[]{:S(2)}) %copy-start.2) | copy-done | bytes 2097176
  61.3 1.6 %copy-done.5 = f32[4096,128]{1,0:T(8,128)S(1)} copy-done((f32[4096,128]{1,0:T(8,128)S(1)}, f32[4096,128]{1,0:T(8,128)}, u32[]{:S(2)}) %copy-start.5) | copy-done | bytes 2097176
  62.9 1.6 %copy-done.7 = f32[4096,128]{1,0:T(8,128)S(1)} copy-done((f32[4096,128]{1,0:T(8,128)S(1)}, f32[4096,128]{1,0:T(8,128)}, u32[]{:S(2)}) %copy-start.7) | copy-done | bytes 2097176
  64.5 5.5 %detect.2.refs_0_ = f32[256,256]{1,0:T(8,128)S(1)} custom-call(bf16[16,4,192,128]{3,2,1,0:T(8,128)(2,1)S(1)} %bitcast.7, bf16[1024,128]{1,0:T(8,128)(2,1)S(1)} %slice_select_fusion.refs_1_, s32[4,3072]{1,0:T(4,128)S(1)} %pad_add_fusion.refs_2_.refs_3_, bf16[128,128]{1,0:T(8,128)(2,1)S(1)} %get-tuple-element.10.refs_3_.refs_4_, ...), custom_call_target="tpu_custom_call" | custom-call | flops 1073741824 | bytes 16777216 | tf_op jit(solution)/shard_map/detect/pallas_call | solution.py:289
  70.0 5.5 %detect.3 = bf16[256,256]{1,0:T(8,128)(2,1)S(1)} custom-call(f32[256,256]{1,0:T(8,128)S(1)} %detect.2.refs_0_, bf16[16,4,192,128]{3,2,1,0:T(8,128)(2,1)S(1)} %bitcast.8, bf16[1024,128]{1,0:T(8,128)(2,1)S(1)} %collective-permute-done.3.refs_2_, s32[4,3072]{1,0:T(4,128)S(1)} %pad_add_fusion.refs_2_.refs_3_, ...), custom_call_target="tpu_custom_call" | custom-call | flops 1073741824 | bytes 16777216 | tf_op jit(solution)/shard_map/detect/pallas_call | solution.py:289
  75.5 31.6 %all_to_all.10 = bf16[8,32,256]{2,1,0:T(8,128)(2,1)S(1)} all-to-all(bf16[8,32,256]{2,1,0:T(8,128)(2,1)S(1)} %bitcast.9), channel_id=1, replica_groups=mesh['chan'=16,'zh'=8,'zl'=2,'xh'=2] {'zh'}, dimensions={0} | all-to-all | bytes 262144 | tf_op jit(solution)/shard_map/all_to_all | solution.py:335
  107.1 0.6 mul.191
  (36 shorter events, 0.4 us)
Async XLA Ops:
  4.1 10.2 %copy-start.8 = (s32[3072]{0:T(1024)S(1)}, s32[3072]{0:T(1024)}, u32[]{:S(2)}) copy-start(s32[3072]{0:T(1024)} %param.7) | copy-start | bytes 36868
  4.1 10.2 %copy-start.9 = (s32[3072]{0:T(1024)S(1)}, s32[3072]{0:T(1024)}, u32[]{:S(2)}) copy-start(s32[3072]{0:T(1024)} %param.8) | copy-start | bytes 36868
  4.1 21.3 %copy-start.10 = (f32[128]{0:T(128)S(1)}, f32[128]{0:T(128)}, u32[]{:S(2)}) copy-start(f32[128]{0:T(128)} %param.6) | copy-start | bytes 1540
  4.1 49.3 %all-to-all-start = ((bf16[64,192,128]{2,1,0:T(8,128)(2,1)}), bf16[64,192,128]{2,1,0:T(8,128)(2,1)S(1)}, u32[]{:S(2)}, u32[]{:S(2)}) async-start(bf16[64,192,128]{2,1,0:T(8,128)(2,1)} %pack.1), calls=%async_computation | async-start | bytes 6291456 | tf_op jit(solution)/shard_map/all_to_all | solution.py:316
  14.6 36.5 %collective-permute-start.1 = (s32[1,3072]{1,0:T(1,128)S(1)}, s32[1,3072]{1,0:T(1,128)S(1)}, u32[]{:S(2)}, u32[]{:S(2)}) collective-permute-start(s32[1,3072]{1,0:T(1,128)S(1)} %reshape.70), channel_id=1, source_target_pairs={{0,2},{2,0},{1,3},{3,1},{4,6},{6,4},{5,7},{7,5},{8,10},{10,8},{9,1... | collective-permute-start | bytes 36872 | tf_op jit(solution)/shard_map/ppermute | solution.py:305
  18.0 35.4 %collective-permute-start.2 = (s32[1,3072]{1,0:T(1,128)S(1)}, s32[1,3072]{1,0:T(1,128)S(1)}, u32[]{:S(2)}, u32[]{:S(2)}) collective-permute-start(s32[1,3072]{1,0:T(1,128)S(1)} %reshape.70), channel_id=1, source_target_pairs={{0,3},{1,2},{2,1},{3,0},{4,7},{5,6},{6,5},{7,4},{8,11},{9,10},{10,... | collective-permute-start | bytes 36872 | tf_op jit(solution)/shard_map/ppermute | solution.py:306
  22.9 28.2 %collective-permute-start = (s32[1,3072]{1,0:T(1,128)S(1)}, s32[1,3072]{1,0:T(1,128)S(1)}, u32[]{:S(2)}, u32[]{:S(2)}) collective-permute-start(s32[1,3072]{1,0:T(1,128)S(1)} %reshape.70), channel_id=1, source_target_pairs={{0,1},{1,0},{2,3},{3,2},{4,5},{5,4},{6,7},{7,6},{8,9},{9,8},{10,11... | collective-permute-start | bytes 36872 | tf_op jit(solution)/shard_map/ppermute | solution.py:304
  37.2 1.4 %copy-start.6 = (f32[4096,128]{1,0:T(8,128)}, f32[4096,128]{1,0:T(8,128)S(1)}, u32[]{:S(2)}) copy-start(f32[4096,128]{1,0:T(8,128)S(1)} %get-tuple-element.8.refs_7_.refs_8_) | copy-start | bytes 6291460
  39.2 1.3 %copy-start.4 = (f32[4096,128]{1,0:T(8,128)}, f32[4096,128]{1,0:T(8,128)S(1)}, u32[]{:S(2)}) copy-start(f32[4096,128]{1,0:T(8,128)S(1)} %get-tuple-element.7.refs_6_.refs_7_) | copy-start | bytes 6291460
  53.5 16.5 %collective-permute-start.3 = (bf16[1024,128]{1,0:T(8,128)(2,1)S(1)}, bf16[1024,128]{1,0:T(8,128)(2,1)S(1)}, u32[]{:S(2)}, u32[]{:S(2)}) collective-permute-start(bf16[1024,128]{1,0:T(8,128)(2,1)S(1)} %slice_select_fusion.refs_1_), channel_id=1, source_target_pairs={{0,4},{4,8},{8,12},{12,16},{16,20},{20,24},{24,28},{1,5},{5,9},{9,... | collective-permute-start | bytes 786440 | tf_op jit(solution)/shard_map/ppermute | solution.py:331
  58.1 1.6 %copy-start = (f32[4096,128]{1,0:T(8,128)S(1)}, f32[4096,128]{1,0:T(8,128)}, u32[]{:S(2)}) copy-start(f32[4096,128]{1,0:T(8,128)} %get-tuple-element.17.refs_9_.refs_10_) | copy-start | bytes 6291460
  59.7 1.6 %copy-start.2 = (f32[4096,128]{1,0:T(8,128)S(1)}, f32[4096,128]{1,0:T(8,128)}, u32[]{:S(2)}) copy-start(f32[4096,128]{1,0:T(8,128)} %get-tuple-element.18.refs_8_.refs_9_) | copy-start | bytes 6291460
  61.3 1.6 %copy-start.5 = (f32[4096,128]{1,0:T(8,128)S(1)}, f32[4096,128]{1,0:T(8,128)}, u32[]{:S(2)}) copy-start(f32[4096,128]{1,0:T(8,128)} %copy-done.4) | copy-start | bytes 6291460
  62.9 1.6 %copy-start.7 = (f32[4096,128]{1,0:T(8,128)S(1)}, f32[4096,128]{1,0:T(8,128)}, u32[]{:S(2)}) copy-start(f32[4096,128]{1,0:T(8,128)} %copy-done.6) | copy-start | bytes 6291460
  64.5 5.5 %copy-start.1 = (f32[4096,128]{1,0:T(8,128)S(1)}, f32[4096,128]{1,0:T(8,128)}, u32[]{:S(2)}) copy-start(f32[4096,128]{1,0:T(8,128)} %get-tuple-element.17.refs_9_.refs_10_) | copy-start | bytes 6291460
  64.5 5.5 %copy-start.3 = (f32[4096,128]{1,0:T(8,128)S(1)}, f32[4096,128]{1,0:T(8,128)}, u32[]{:S(2)}) copy-start(f32[4096,128]{1,0:T(8,128)} %get-tuple-element.18.refs_8_.refs_9_) | copy-start | bytes 6291460
